TPU v7x, 32 devices: a whole 2x2x4 slice. The times are simulated.
32 devices in a mesh: groups: 1, row: 8 (over z, x), col: 4 (over y, core).
Axes of the slice: x: 2, y: 2, z: 4, core: 2. Of those that a mesh axis runs over, the one named last changes fastest.
Arguments:
- features: bfloat16 [512, 1536], P(('groups', 'row', 'col')), may hold values from -6 to 6
- first_weight: bfloat16 [1536, 48], replicated, may hold values from -0.15625 to 0.15625
- second_weight: bfloat16 [1536, 48], replicated, may hold values from -0.15625 to 0.15625
- conv_kernel: bfloat16 [3, 3, 48, 48], replicated, may hold values from -0.3125 to 0.3125
- conv_bias: float32 [48], replicated, may hold values from -3 to 3
- dilated_kernels: bfloat16 [3, 3, 3, 48, 48], replicated, may hold values from -0.3125 to 0.3125
- mixing_weights: bfloat16 [3, 48, 48], replicated, may hold values from -0.875 to 0.875
Outputs:
- contact_map: bfloat16 [48, 512, 512], P('groups', 'row', 'col')
All inputs are finite; a program needn't handle non-finite values.
Results may differ from a plain program's by a relative error of at most 0.0065.
Values may be sent and summed in bfloat16 or wider, within the bound.
No kernel may reach another device: no remote copies, remote signals or barrier semaphores. Data moves between devices by JAX's collectives and lax.ppermute only.
A program may use at most 128 MiB of HBM per device.

v0:
```python
import functools

import jax
import jax.numpy as jnp
from jax import lax
from jax.experimental import pallas as pl
from jax.experimental.pallas import tpu as pltpu
from jax.sharding import PartitionSpec as P

MARGIN = 16
GROUP = 8
LANES = 128
FAR = -1e30
SPREADS = (2, 4, 8)


def haloed(p_ref, start, count, bins):
    before = pl.multiple_of(jnp.maximum(start - MARGIN, 0), MARGIN)
    after = pl.multiple_of(jnp.minimum(start + count, bins - MARGIN), MARGIN)
    top = p_ref[pl.ds(before, MARGIN), :].astype(jnp.float32)
    mid = p_ref[pl.ds(pl.multiple_of(start, MARGIN), count), :].astype(jnp.float32)
    low = p_ref[pl.ds(after, MARGIN), :].astype(jnp.float32)
    top = jnp.where(start > 0, top, FAR)
    low = jnp.where(start + count < bins, low, FAR)
    return jnp.concatenate([top, mid, low], axis=0)


def trunk(
    rows_tile, cols_tile, bins, channels,
    pos_ref, p_ref, w1_ref, wd_ref, wm_ref, bias_ref, hi_ref, out_ref,
    rb, cpat, state, act, sq, sh, oscr,
):
    width = cols_tile + 2 * MARGIN
    height = rows_tile + 2 * MARGIN
    step = GROUP * width
    period = 4 * width
    tiles = period // LANES
    both = 2 * channels
    rows_t = jnp.transpose(haloed(p_ref, pos_ref[0], rows_tile, bins))
    cols_t = jnp.transpose(haloed(p_ref, pos_ref[1], cols_tile, bins))
    rb[0] = jnp.zeros((both, LANES), jnp.bfloat16)
    rb[height + 1] = jnp.zeros((both, LANES), jnp.bfloat16)
    for i in range(height):
        rb[i + 1] = jnp.broadcast_to(rows_t[:, i : i + 1], (both, LANES)).astype(jnp.bfloat16)
    cols_s = jnp.concatenate([cols_t[channels:], cols_t[:channels]], axis=0)
    cols_p = jnp.concatenate([cols_s] * 4, axis=1)
    for q in (-1, 0, 1):
        cpat[q + 1] = (pltpu.roll(cols_p, (-q) % period, axis=1) if q else cols_p).astype(jnp.bfloat16)

    lane = lax.broadcasted_iota(jnp.int32, (both, LANES), 1)
    bias = jnp.broadcast_to(bias_ref[...], (channels, 2 * LANES))
    zero = jnp.bfloat16(0)

    def clipped(value, off, size):
        hi = hi_ref[:, pl.ds(off, size)]
        hi = jnp.concatenate([hi] * (channels // 16), axis=0)
        return jnp.minimum(jnp.maximum(value, 0.0).astype(jnp.bfloat16), hi)

    def first(g, _):
        for pair in range(step // (2 * LANES)):
            halves = []
            for t in (2 * pair, 2 * pair + 1):
                base = 4 * (t // tiles)
                t = t % tiles
                r0 = (t * LANES) // width
                r1 = (t * LANES + LANES - 1) // width
                split = r1 * width - t * LANES
                pieces = []
                for p in (-1, 0, 1):
                    row = rb[g * GROUP + (base + r0 + p + 1)]
                    if r1 != r0:
                        row = jnp.where(lane < split, row, rb[g * GROUP + (base + r1 + p + 1)])
                    for q in (-1, 0, 1):
                        pieces.append(jnp.maximum(row + cpat[q + 1, :, t * LANES : (t + 1) * LANES], zero))
                halves.append(jnp.concatenate(pieces, axis=0))
            x = jnp.concatenate(halves, axis=1)
            off = pl.multiple_of(g * step + pair * 2 * LANES, LANES)
            st = 0.5 * jnp.dot(w1_ref[...], x, preferred_element_type=jnp.float32) + bias
            state[:, pl.ds(off, 2 * LANES)] = st
            act[:, pl.ds(off + LANES, 2 * LANES)] = clipped(st, off, 2 * LANES)
        return 0

    lax.fori_loop(0, height // GROUP, first, 0)

    edge = 0
    for block, spread in enumerate(SPREADS):
        shift = spread * width
        ragged = shift % LANES
        rest = (-shift) % LANES
        assert ragged == rest

        def spreadout(g, _, edge=edge, spread=spread, ragged=ragged):
            off = pl.multiple_of(g * step + edge * width, LANES)
            window = act[:, pl.ds(off, step + 2 * LANES)]
            for q in (-1, 0, 1):
                at = LANES + q * spread
                rows = slice((q + 1) * channels, (q + 2) * channels)
                sq[rows, pl.ds(off, step)] = window[:, at : at + step]
                if ragged:
                    at += ragged
                    sh[rows, pl.ds(off, step)] = window[:, at : at + step]
            return 0

        inner_rows = height - 2 * edge
        lax.fori_loop(0, inner_rows // GROUP, spreadout, 0)
        edge = 4 if spread == 2 else 2 * spread
        last = block == len(SPREADS) - 1
        side = sh if ragged else sq

        def dilated(g, _, edge=edge, block=block, shift=shift, ragged=ragged, side=side, last=last):
            outs = []
            for pair in range(step // (2 * LANES)):
                size = 2 * LANES
                off = pl.multiple_of(g * step + (edge * width + pair * size), LANES)
                x = jnp.concatenate(
                    [
                        side[:, pl.ds(pl.multiple_of(off - shift - ragged, LANES), size)],
                        sq[:, pl.ds(off, size)],
                        side[:, pl.ds(pl.multiple_of(off + shift - ragged, LANES), size)],
                    ],
                    axis=0,
                )
                inner = jnp.dot(wd_ref[block], x, preferred_element_type=jnp.float32)
                gated = jnp.maximum(inner, 0.0).astype(jnp.bfloat16)
                st = state[:, pl.ds(off, size)] + jnp.dot(
                    wm_ref[block], gated, preferred_element_type=jnp.float32
                )
                if last:
                    outs.append(st)
                else:
                    state[:, pl.ds(off, size)] = st
                    act[:, pl.ds(off + LANES, size)] = clipped(st, off, size)
            if last:
                whole = jnp.concatenate(outs, axis=1)
                for k in range(GROUP):
                    at = k * width + MARGIN
                    oscr[pl.ds(k, channels, stride=GROUP), :] = whole[:, at : at + LANES]
                rows = pl.ds(pl.multiple_of(g * GROUP, GROUP), GROUP)
                out_ref[:, rows, :] = oscr[...].reshape(channels, GROUP, LANES).astype(jnp.bfloat16)
            return 0

        lax.fori_loop(0, (height - 2 * edge) // GROUP, dilated, 0)


def local(
    features, first_weight, second_weight, conv_kernel, conv_bias, dilated_kernels, mixing_weights
):
    channels = first_weight.shape[1]
    row_count, col_count = lax.axis_size("row"), lax.axis_size("col")
    devices = row_count * col_count
    mine = jnp.concatenate(
        [
            jnp.dot(features, first_weight, preferred_element_type=jnp.float32),
            jnp.dot(features, second_weight, preferred_element_type=jnp.float32),
        ],
        1,
    ).astype(jnp.bfloat16)
    bins = features.shape[0] * devices
    both = lax.all_to_all(
        jnp.broadcast_to(mine[None], (devices,) + mine.shape), ("row", "col"), 0, 0
    ).reshape(bins, 2 * channels)
    rows_tile = bins // row_count
    cols_tile = bins // col_count
    height, width = rows_tile + 2 * MARGIN, cols_tile + 2 * MARGIN
    row_start = lax.axis_index("row") * rows_tile
    col_start = lax.axis_index("col") * cols_tile
    pos = jnp.stack([row_start, col_start]).astype(jnp.int32)
    row_ids = row_start - MARGIN + jnp.arange(height, dtype=jnp.int32)
    col_ids = col_start - MARGIN + jnp.arange(width, dtype=jnp.int32)
    inside = ((row_ids >= 0) & (row_ids < bins))[:, None] & ((col_ids >= 0) & (col_ids < bins))[None]
    hi = jnp.broadcast_to(
        jnp.where(inside, jnp.inf, 0.0).astype(jnp.bfloat16).reshape(1, height * width),
        (16, height * width),
    )
    straight = jnp.transpose(conv_kernel, (2, 0, 1, 3))
    swapped = jnp.transpose(conv_kernel, (2, 1, 0, 3))
    w1 = jnp.stack([straight, swapped], axis=3).reshape(channels, 18 * channels)
    wd = jnp.transpose(dilated_kernels, (0, 3, 1, 2, 4)).reshape(3, channels, 9 * channels)
    lanes = height * width
    vmem = pl.BlockSpec(memory_space=pltpu.VMEM)
    return pl.pallas_call(
        functools.partial(trunk, rows_tile, cols_tile, bins, channels),
        out_shape=jax.ShapeDtypeStruct((channels, rows_tile, cols_tile), jnp.bfloat16),
        in_specs=[pl.BlockSpec(memory_space=pltpu.SMEM)] + [vmem] * 6,
        out_specs=vmem,
        scratch_shapes=[
            pltpu.VMEM((height + 2, 2 * channels, LANES), jnp.bfloat16),
            pltpu.VMEM((3, 2 * channels, 4 * width), jnp.bfloat16),
            pltpu.VMEM((channels, lanes), jnp.float32),
            pltpu.VMEM((channels, lanes + 2 * LANES), jnp.bfloat16),
            pltpu.VMEM((3 * channels, lanes), jnp.bfloat16),
            pltpu.VMEM((3 * channels, lanes), jnp.bfloat16),
            pltpu.VMEM((channels * GROUP, LANES), jnp.float32),
        ],
        compiler_params=pltpu.CompilerParams(vmem_limit_bytes=56 << 20),
        name="trunk",
    )(pos, both, w1, wd, mixing_weights, conv_bias[:, None], hi)


def solution(mesh):
    in_specs = (P(("groups", "row", "col"), None), P(), P(), P(), P(), P(), P())
    out_specs = P("groups", "row", "col")
    return jax.shard_map(local, mesh=mesh, in_specs=in_specs, out_specs=out_specs, check_vma=False)
```

profile of v0, /device:TPU:0, one launch (start us, length us, event | category | flops | bytes accessed | tf_op | source)
XLA Modules:
  0.0 63.2 jit_solution(11115977625617647252)
XLA Ops:
  0.0 0.0 copy-start
  0.0 0.0 copy-start.4
  0.0 0.0 copy-start.5
  0.0 0.9 %copy-done = bf16[1536,48]{0,1:T(8,128)(2,1)S(1)} copy-done((bf16[1536,48]{0,1:T(8,128)(2,1)S(1)}, bf16[1536,48]{0,1:T(8,128)(2,1)}, u32[]{:S(2)}) %copy-start) | copy-done | bytes 147480
  0.9 0.9 %convolution_convert_fusion.1 = bf16[16,48]{1,0:T(8,128)(2,1)S(1)} fusion(bf16[16,1536]{1,0:T(8,128)(2,1)} %param.7, bf16[1536,48]{0,1:T(8,128)(2,1)S(1)} %copy-done), kind=kOutput, calls=%fused_computation.1 | convolution fusion | flops 2360064 | bytes 198144 | tf_op jit(solution)/shard_map/dot_general | solution.py:153
  1.8 0.0 copy-done.4
  1.8 0.0 copy-done.5
  1.8 0.2 convolution_convert_fusion
  2.0 0.1 pad_maximum_fusion.1
  2.1 0.7 %broadcast_in_dim.24 = bf16[32,16,96]{2,1,0:T(8,128)(2,1)} broadcast(bf16[16,96]{1,0:T(8,128)(2,1)S(1)} %pad_maximum_fusion.1), dimensions={1,2} | broadcast | bytes 101376 | tf_op jit(solution)/shard_map/broadcast_in_dim | solution.py:160
  2.8 0.0 copy-start.6
  2.8 7.3 %all-to-all-start = ((bf16[32,16,96]{2,1,0:T(8,128)(2,1)}), bf16[32,16,96]{2,1,0:T(8,128)(2,1)S(1)}, u32[]{:S(2)}, u32[]{:S(2)}) async-start(bf16[32,16,96]{2,1,0:T(8,128)(2,1)} %broadcast_in_dim.24), calls=%async_computation | async-start | bytes 262144 | tf_op jit(solution)/shard_map/all_to_all | solution.py:159
  10.1 0.0 copy-start.2
  10.1 0.0 copy-done.6
  10.2 0.7 %copy.15.bias_ref = f32[48,1]{1,0:T(8,128)} copy(f32[48,1]{0,1:T(1,128)S(1)} %bitcast.21) | data formatting | bytes 384 | tf_op jit(solution)/shard_map/broadcast_in_dim | solution.py:197
  10.8 0.1 select_convert_fusion
  10.9 0.1 convert_element_type.16
  11.1 0.0 copy-done.2
  11.1 0.1 pad_maximum_fusion
  11.1 0.0 copy-start.3
  11.2 0.2 copy.13
  11.3 0.8 %reshape.60.w1_ref = bf16[48,864]{1,0:T(8,128)(2,1)} reshape(bf16[48,3,3,2,48]{4,3,2,1,0:T(2,128)(2,1)S(1)} %copy.13) | data formatting | bytes 165888 | tf_op jit(solution)/shard_map/reshape | solution.py:177
  12.2 0.0 copy-done.3
  12.2 0.2 copy.14
  12.3 0.9 %reshape.61.wd_ref = bf16[3,48,432]{2,1,0:T(8,128)(2,1)} reshape(bf16[3,48,3,3,48]{4,3,2,1,0:T(4,128)(2,1)S(1)} %copy.14) | data formatting | bytes 248832 | tf_op jit(solution)/shard_map/reshape | solution.py:178
  13.2 0.7 %pad_add_fusion.pos_ref = s32[2]{0:T(128)} fusion(s32[1]{0:T(128)} %bitcast.1, s32[1]{0:T(128)} %bitcast), kind=kLoop, calls=%fused_computation.8 | loop fusion | flops 2 | bytes 16 | tf_op jit(solution)/shard_map/stack | solution.py:167
  13.9 4.4 %all-to-all-done = bf16[32,16,96]{2,1,0:T(8,128)(2,1)S(1)} async-done(((bf16[32,16,96]{2,1,0:T(8,128)(2,1)}), bf16[32,16,96]{2,1,0:T(8,128)(2,1)S(1)}, u32[]{:S(2)}, u32[]{:S(2)}) %all-to-all-start) | async-done | bytes 98336 | tf_op jit(solution)/shard_map/all_to_all | solution.py:159
  18.3 0.0 copy-start.1
  18.3 0.8 %broadcast_in_dim.28.hi_ref = bf16[16,15360]{1,0:T(8,128)(2,1)} broadcast(bf16[15360]{0:T(1024)(128)(2,1)S(1)} %convert_element_type.16), dimensions={1} | broadcast | bytes 522240 | tf_op jit(solution)/shard_map/broadcast_in_dim | solution.py:171
  19.2 0.0 copy-done.1
  19.2 44.0 %trunk.1 = bf16[48,64,128]{2,1,0:T(8,128)(2,1)} custom-call(s32[2]{0:T(128)} %pad_add_fusion.pos_ref, bf16[512,96]{1,0:T(8,128)(2,1)} %bitcast.17, bf16[48,864]{1,0:T(8,128)(2,1)} %reshape.60.w1_ref, bf16[3,48,432]{2,1,0:T(8,128)(2,1)} %reshape.61.wd_ref, bf16[3,48,48]{2,1,0:T(8,128)(2,1)} %wm_ref.1, f32[48,1]{1,0:T(8,128)} %copy.15.bias_ref, ...), custom_call_target="tpu_custom_call" | custom-call | tf_op jit(solution)/shard_map/trunk/pallas_call | solution.py:181
  (3 shorter events, 0.0 us)
Async XLA Ops:
  0.0 0.9 %copy-start = (bf16[1536,48]{0,1:T(8,128)(2,1)S(1)}, bf16[1536,48]{0,1:T(8,128)(2,1)}, u32[]{:S(2)}) copy-start(bf16[1536,48]{0,1:T(8,128)(2,1)} %param.8) | copy-start | bytes 442372
  0.0 1.8 %copy-start.4 = (bf16[16,1536]{1,0:T(8,128)(2,1)S(1)}, bf16[16,1536]{1,0:T(8,128)(2,1)}, u32[]{:S(2)}) copy-start(bf16[16,1536]{1,0:T(8,128)(2,1)} %param.7) | copy-start | bytes 147460
  0.0 1.8 %copy-start.5 = (bf16[1536,48]{0,1:T(8,128)(2,1)S(1)}, bf16[1536,48]{0,1:T(8,128)(2,1)}, u32[]{:S(2)}) copy-start(bf16[1536,48]{0,1:T(8,128)(2,1)} %param.9) | copy-start | bytes 442372
  2.8 7.4 %copy-start.6 = (f32[48]{0:T(128)S(1)}, f32[48]{0:T(128)}, u32[]{:S(2)}) copy-start(f32[48]{0:T(128)} %param.11) | copy-start | bytes 580
  2.8 15.5 %all-to-all-start = ((bf16[32,16,96]{2,1,0:T(8,128)(2,1)}), bf16[32,16,96]{2,1,0:T(8,128)(2,1)S(1)}, u32[]{:S(2)}, u32[]{:S(2)}) async-start(bf16[32,16,96]{2,1,0:T(8,128)(2,1)} %broadcast_in_dim.24), calls=%async_computation | async-start | bytes 262144 | tf_op jit(solution)/shard_map/all_to_all | solution.py:159
  10.1 1.0 %copy-start.2 = (bf16[3,3,48,48]{3,2,1,0:T(8,128)(2,1)S(1)}, bf16[3,3,48,48]{3,2,1,0:T(8,128)(2,1)}, u32[]{:S(2)}) copy-start(bf16[3,3,48,48]{3,2,1,0:T(8,128)(2,1)} %param.10) | copy-start | bytes 124420
  11.1 1.0 %copy-start.3 = (bf16[3,3,3,48,48]{4,3,2,1,0:T(8,128)(2,1)S(1)}, bf16[3,3,3,48,48]{4,3,2,1,0:T(8,128)(2,1)}, u32[]{:S(2)}) copy-start(bf16[3,3,3,48,48]{4,3,2,1,0:T(8,128)(2,1)} %param.12) | copy-start | bytes 373252
  18.3 0.8 %copy-start.1 = (bf16[32,16,96]{2,1,0:T(8,128)(2,1)}, bf16[32,16,96]{2,1,0:T(8,128)(2,1)S(1)}, u32[]{:S(2)}) copy-start(bf16[32,16,96]{2,1,0:T(8,128)(2,1)S(1)} %all-to-all-done) | copy-start | bytes 294916
where the time goes:
time: 63.4 us; the launch traced here: 63.2 us
  Pallas kernels  44 us (69%)
  starting transfers between devices  7.3 us (12%)
  local copies, waits for them, and re-layouts  5.36 us (8%)
  waiting for transfers between devices  4.42 us (7%)
  matrix products  1.09 us (2%)
  other arithmetic  0.91 us (1%)
    pallas_call x1, Pallas kernels, local(): pl.pallas_call(functools.partial(trunk, rows_tile, cols_tile, bins, chann...  44 us
    all_to_all x1, starting transfers between devices, local(): lax.all_to_all(jnp.broadcast_to(mine[None], (devices,) + mine.shape), ('r...  7.3 us
    all_to_all x1, waiting for transfers between devices, local(): lax.all_to_all(jnp.broadcast_to(mine[None], (devices,) + mine.shape), ('r...  4.42 us
  transfers between devices with their start and end apart: 1, of which 1 were waited for; matrix products, arithmetic and copies ran while one was open for 6% of the time, Pallas kernels for 0%

commit v1 on v0

v1 whole, which is shorter than its diff:
```python
import functools

import jax
import jax.numpy as jnp
from jax import lax
from jax.experimental import pallas as pl
from jax.experimental.pallas import tpu as pltpu
from jax.sharding import PartitionSpec as P

MARGIN = 16
GROUP = 16
LANES = 128
FAR = -1e30
SPREADS = (2, 4, 8)


def haloed(p_ref, start, count, bins):
    before = pl.multiple_of(jnp.maximum(start - MARGIN, 0), MARGIN)
    after = pl.multiple_of(jnp.minimum(start + count, bins - MARGIN), MARGIN)
    top = p_ref[pl.ds(before, MARGIN), :].astype(jnp.float32)
    mid = p_ref[pl.ds(pl.multiple_of(start, MARGIN), count), :].astype(jnp.float32)
    low = p_ref[pl.ds(after, MARGIN), :].astype(jnp.float32)
    top = jnp.where(start > 0, top, FAR)
    low = jnp.where(start + count < bins, low, FAR)
    return jnp.concatenate([top, mid, low], axis=0)


def trunk(
    rows_tile, cols_tile, bins, channels,
    pos_ref, p_ref, w1_ref, wd_ref, wm_ref, bias_ref, hi_ref, out_ref,
    rb, cpat, state, act_a, act_b, side, tail, oscr,
):
    width = cols_tile + 2 * MARGIN
    height = rows_tile + 2 * MARGIN
    period = 4 * width
    tiles = period // LANES
    both = 2 * channels
    rows_t = jnp.transpose(haloed(p_ref, pos_ref[0], rows_tile, bins))
    cols_t = jnp.transpose(haloed(p_ref, pos_ref[1], cols_tile, bins))
    rb[0] = jnp.zeros((both, LANES), jnp.bfloat16)
    rb[height + 1] = jnp.zeros((both, LANES), jnp.bfloat16)
    for i in range(height):
        rb[i + 1] = jnp.broadcast_to(rows_t[:, i : i + 1], (both, LANES)).astype(jnp.bfloat16)
    cols_s = jnp.concatenate([cols_t[channels:], cols_t[:channels]], axis=0)
    cpat[...] = jnp.concatenate([cols_s] * 4, axis=1).astype(jnp.bfloat16)

    lane = lax.broadcasted_iota(jnp.int32, (both, LANES), 1)
    half = lax.broadcasted_iota(jnp.int32, (channels, LANES), 1) < LANES // 2
    zero = jnp.bfloat16(0)

    def chunks(first_row, count, body):
        full = count // GROUP
        lax.fori_loop(0, full, lambda g, c: body(g * GROUP + first_row, GROUP) or c, 0)
        if count % GROUP:
            body(first_row + full * GROUP, count % GROUP)

    def clipped(value, off, size):
        return jnp.minimum(jnp.maximum(value, 0.0), hi_ref[:, pl.ds(off, size)]).astype(jnp.bfloat16)

    def gathered(z, spread):
        size = z.shape[1]
        return (
            z[channels : 2 * channels]
            + pltpu.roll(z[:channels], spread, axis=1)
            + pltpu.roll(z[2 * channels :], size - spread, axis=1)
        )

    def first(row0, rows):
        size = rows * width
        off = pl.multiple_of(row0 * width, LANES)
        zs = []
        for pair in range(size // (2 * LANES)):
            halves = []
            for t in (2 * pair, 2 * pair + 1):
                base = 4 * (t // tiles)
                t = t % tiles
                r0 = (t * LANES) // width
                r1 = (t * LANES + LANES - 1) // width
                split = r1 * width - t * LANES
                col = cpat[:, t * LANES : (t + 1) * LANES]
                pieces = []
                for p in (-1, 0, 1):
                    row = rb[row0 + (base + r0 + p + 1)]
                    if r1 != r0:
                        row = jnp.where(lane < split, row, rb[row0 + (base + r1 + p + 1)])
                    pieces.append(jnp.maximum(row + col, zero))
                halves.append(jnp.concatenate(pieces, axis=0))
            x = jnp.concatenate(halves, axis=1)
            zs.append(jnp.dot(w1_ref[...], x, preferred_element_type=jnp.float32))
        st = 0.5 * gathered(jnp.concatenate(zs, axis=1), 1) + bias_ref[...]
        act = clipped(st, off, size)
        turned = pltpu.roll(act.astype(jnp.float32), LANES // 2, axis=1).astype(jnp.bfloat16)
        ahead = jnp.where(half, tail[...], turned[:, :LANES])
        state[:, pl.ds(off, size)] = st
        act_a[:, pl.ds(off, size)] = act
        side[:, pl.ds(off, size)] = jnp.concatenate([ahead, turned[:, LANES:]], axis=1)
        tail[...] = turned[:, :LANES]

    tail[...] = jnp.zeros_like(tail)
    chunks(0, height, first)

    edge = 0
    src, dst = act_a, act_b
    for block, spread in enumerate(SPREADS):
        shift = spread * width
        ragged = shift % LANES
        assert ragged in (0, LANES // 2)
        edge = 4 if spread == 2 else 2 * spread
        last = block == len(SPREADS) - 1
        around = side if ragged else src

        def dilated(row0, rows, block=block, spread=spread, shift=shift, ragged=ragged, src=src, dst=dst,
                    around=around, last=last, edge=edge):
            size = rows * width
            off = pl.multiple_of(row0 * width, LANES)
            x = jnp.concatenate(
                [
                    around[:, pl.ds(pl.multiple_of(off - shift + ragged, LANES), size)],
                    src[:, pl.ds(off, size)],
                    around[:, pl.ds(pl.multiple_of(off + shift + ragged, LANES), size)],
                ],
                axis=0,
            )
            z = jnp.dot(wd_ref[block], x, preferred_element_type=jnp.float32)
            gated = jnp.maximum(gathered(z, spread), 0.0).astype(jnp.bfloat16)
            st = state[:, pl.ds(off, size)] + jnp.dot(
                wm_ref[block], gated, preferred_element_type=jnp.float32
            )
            if not last:
                state[:, pl.ds(off, size)] = st
                dst[:, pl.ds(off, size)] = clipped(st, off, size)
                return
            for k in range(rows):
                at = k * width + MARGIN
                oscr[pl.ds(k, channels, stride=GROUP), :] = st[:, at : at + LANES]
            place = pl.ds(pl.multiple_of(row0 - MARGIN, GROUP), GROUP)
            out_ref[:, place, :] = oscr[...].reshape(channels, GROUP, LANES).astype(jnp.bfloat16)

        chunks(edge, height - 2 * edge, dilated)
        src, dst = dst, src


def call_trunk(rows_tile, cols_tile, bins, channels, *operands):
    height, width = rows_tile + 2 * MARGIN, cols_tile + 2 * MARGIN
    lanes = height * width
    vmem = pl.BlockSpec(memory_space=pltpu.VMEM)
    return pl.pallas_call(
        functools.partial(trunk, rows_tile, cols_tile, bins, channels),
        out_shape=jax.ShapeDtypeStruct((channels, rows_tile, cols_tile), jnp.bfloat16),
        in_specs=[pl.BlockSpec(memory_space=pltpu.SMEM)] + [vmem] * 6,
        out_specs=vmem,
        scratch_shapes=[
            pltpu.VMEM((height + 2, 2 * channels, LANES), jnp.bfloat16),
            pltpu.VMEM((2 * channels, 4 * width), jnp.bfloat16),
            pltpu.VMEM((channels, lanes), jnp.float32),
            pltpu.VMEM((channels, lanes), jnp.bfloat16),
            pltpu.VMEM((channels, lanes), jnp.bfloat16),
            pltpu.VMEM((channels, lanes), jnp.bfloat16),
            pltpu.VMEM((channels, LANES), jnp.bfloat16),
            pltpu.VMEM((channels * GROUP, LANES), jnp.float32),
        ],
        compiler_params=pltpu.CompilerParams(vmem_limit_bytes=56 << 20),
        name="trunk",
    )(*operands)


def local(
    features, first_weight, second_weight, conv_kernel, conv_bias, dilated_kernels, mixing_weights
):
    channels = first_weight.shape[1]
    row_count, col_count = lax.axis_size("row"), lax.axis_size("col")
    devices = row_count * col_count
    mine = jnp.concatenate(
        [
            jnp.dot(features, first_weight, preferred_element_type=jnp.float32),
            jnp.dot(features, second_weight, preferred_element_type=jnp.float32),
        ],
        1,
    ).astype(jnp.bfloat16)
    bins = features.shape[0] * devices
    both = lax.all_to_all(
        jnp.broadcast_to(mine[None], (devices,) + mine.shape), ("row", "col"), 0, 0
    ).reshape(bins, 2 * channels)
    rows_tile = bins // row_count
    cols_tile = bins // col_count
    height, width = rows_tile + 2 * MARGIN, cols_tile + 2 * MARGIN
    row_start = lax.axis_index("row") * rows_tile
    col_start = lax.axis_index("col") * cols_tile
    pos = jnp.stack([row_start, col_start]).astype(jnp.int32)
    row_ids = row_start - MARGIN + jnp.arange(height, dtype=jnp.int32)
    col_ids = col_start - MARGIN + jnp.arange(width, dtype=jnp.int32)
    inside = ((row_ids >= 0) & (row_ids < bins))[:, None] & ((col_ids >= 0) & (col_ids < bins))[None]
    hi = jnp.where(inside, jnp.inf, 0.0).astype(jnp.float32).reshape(1, height * width)
    straight = jnp.transpose(conv_kernel, (1, 2, 0, 3))
    swapped = jnp.transpose(conv_kernel, (0, 2, 1, 3))
    w1 = jnp.stack([straight, swapped], axis=3).reshape(3 * channels, 6 * channels)
    wd = jnp.transpose(dilated_kernels, (0, 2, 3, 1, 4)).reshape(3, 3 * channels, 3 * channels)
    return call_trunk(
        rows_tile, cols_tile, bins, channels, pos, both, w1, wd, mixing_weights, conv_bias[:, None], hi
    )


def solution(mesh):
    in_specs = (P(("groups", "row", "col"), None), P(), P(), P(), P(), P(), P())
    out_specs = P("groups", "row", "col")
    return jax.shard_map(local, mesh=mesh, in_specs=in_specs, out_specs=out_specs, check_vma=False)
```

time: 63.4 us -> 36.9 us (0.58)
  Pallas kernels: 44 us -> 17.7 us
  waiting for transfers between devices: 4.42 us -> 3.13 us
  local copies, waits for them, and re-layouts: 5.36 us -> 6.51 us
    pallas_call x1, Pallas kernels: 44 us -> 17.7 us  [call_trunk(): pl.pallas_call(functools.partial(trunk, rows_tile, cols_tile, bins, chann...]
    unnamed x15, local copies, waits for them, and re-layouts: 0.94 us -> 2.28 us
    all_to_all x1, waiting for transfers between devices: 4.42 us -> 3.13 us  [local(): lax.all_to_all(jnp.broadcast_to(mine[None], (devices,) + mine.shape), ('r...]
    broadcast_in_dim x1 -> x0, local copies, waits for them, and re-layouts: 0.84 us -> none  [local(): jnp.broadcast_to(jnp.where(inside, jnp.inf, 0.0).astype(jnp.bfloat16).res...]
    select_n x0 -> x1, local copies, waits for them, and re-layouts: none -> 0.76 us  [local(): jnp.where(inside, jnp.inf, 0.0).astype(jnp.float32)]
  transfers between devices with their start and end apart: 1 -> 1, of which waited for: 1 -> 1; matrix products, arithmetic and copies ran while one was open for 6% -> 12% of each run, Pallas kernels for 0% -> 0%
where the time goes in v1:
time: 36.9 us; the launch traced here: 36.6 us
  Pallas kernels  17.7 us (48%)
  starting transfers between devices  7.3 us (20%)
  local copies, waits for them, and re-layouts  6.51 us (18%)
  waiting for transfers between devices  3.13 us (8%)
  matrix products  1.09 us (3%)
  other arithmetic  0.86 us (2%)
    pallas_call x1, Pallas kernels, call_trunk(): pl.pallas_call(functools.partial(trunk, rows_tile, cols_tile, bins, chann...  17.7 us
    all_to_all x1, starting transfers between devices, local(): lax.all_to_all(jnp.broadcast_to(mine[None], (devices,) + mine.shape), ('r...  7.3 us
    all_to_all x1, waiting for transfers between devices, local(): lax.all_to_all(jnp.broadcast_to(mine[None], (devices,) + mine.shape), ('r...  3.13 us
    unnamed x15, local copies, waits for them, and re-layouts  2.28 us
    dot_general x1, matrix products, local(): jnp.dot(features, first_weight, preferred_element_type=jnp.float32)  0.93 us
    reshape x1, local copies, waits for them, and re-layouts, local(): jnp.transpose(dilated_kernels, (0, 2, 3, 1, 4))  0.93 us
    reshape x1, local copies, waits for them, and re-layouts, local(): jnp.stack([straight, swapped], axis=3).reshape(3 * channels, 6 * channels)  0.82 us
    select_n x1, local copies, waits for them, and re-layouts, local(): jnp.where(inside, jnp.inf, 0.0).astype(jnp.float32)  0.76 us
  transfers between devices with their start and end apart: 1, of which 1 were waited for; matrix products, arithmetic and copies ran while one was open for 12% of the time, Pallas kernels for 0%

profile of v1, /device:TPU:0, one launch (start us, length us, event | category | flops | bytes accessed | tf_op | source)
XLA Modules:
  0.0 36.6 jit_solution(3251323712298023706)
XLA Ops:
  0.0 0.0 copy-start
  0.0 0.0 copy-start.4
  0.0 0.0 copy-start.5
  0.0 0.9 %copy-done = bf16[1536,48]{0,1:T(8,128)(2,1)S(1)} copy-done((bf16[1536,48]{0,1:T(8,128)(2,1)S(1)}, bf16[1536,48]{0,1:T(8,128)(2,1)}, u32[]{:S(2)}) %copy-start) | copy-done | bytes 147480
  0.9 0.9 %convolution_convert_fusion.1 = bf16[16,48]{1,0:T(8,128)(2,1)S(1)} fusion(bf16[16,1536]{1,0:T(8,128)(2,1)} %param.7, bf16[1536,48]{0,1:T(8,128)(2,1)S(1)} %copy-done), kind=kOutput, calls=%fused_computation.1 | convolution fusion | flops 2360064 | bytes 198144 | tf_op jit(solution)/shard_map/dot_general | solution.py:175
  1.8 0.0 copy-done.4
  1.8 0.0 copy-done.5
  1.8 0.2 convolution_convert_fusion
  2.0 0.1 pad_maximum_fusion.1
  2.1 0.7 %broadcast_in_dim.19 = bf16[32,16,96]{2,1,0:T(8,128)(2,1)} broadcast(bf16[16,96]{1,0:T(8,128)(2,1)S(1)} %pad_maximum_fusion.1), dimensions={1,2} | broadcast | bytes 101376 | tf_op jit(solution)/shard_map/broadcast_in_dim | solution.py:182
  2.8 7.3 %all-to-all-start = ((bf16[32,16,96]{2,1,0:T(8,128)(2,1)}), bf16[32,16,96]{2,1,0:T(8,128)(2,1)S(1)}, u32[]{:S(2)}, u32[]{:S(2)}) async-start(bf16[32,16,96]{2,1,0:T(8,128)(2,1)} %broadcast_in_dim.19), calls=%async_computation | async-start | bytes 262144 | tf_op jit(solution)/shard_map/all_to_all | solution.py:181
  10.1 0.0 copy-start.6
  10.1 0.6 %copy-done.6 = f32[48]{0:T(128)S(1)} copy-done((f32[48]{0:T(128)S(1)}, f32[48]{0:T(128)}, u32[]{:S(2)}) %copy-start.6) | copy-done | bytes 216
  10.8 0.7 %copy.15.bias_ref = f32[48,1]{1,0:T(8,128)} copy(f32[48,1]{0,1:T(1,128)S(1)} %bitcast.21) | data formatting | bytes 384 | tf_op jit(solution)/shard_map/broadcast_in_dim | solution.py:199
  11.5 0.0 copy-start.2
  11.5 0.1 and_select_fusion
  11.6 0.8 %select_n.15.hi_ref = f32[1,15360]{1,0:T(1,128)} reshape(f32[96,160]{1,0:T(8,128)S(1)} %and_select_fusion) | data formatting | bytes 122880 | tf_op jit(solution)/shard_map/jit(_where)/select_n | solution.py:193
  12.3 0.0 copy-done.2
  12.4 0.1 pad_maximum_fusion
  12.5 0.0 copy-start.3
  12.5 0.2 copy.13
  12.6 0.8 %reshape.68.w1_ref = bf16[144,288]{1,0:T(8,128)(2,1)} reshape(bf16[3,48,3,2,48]{4,3,2,1,0:T(2,128)(2,1)S(1)} %copy.13) | data formatting | bytes 165888 | tf_op jit(solution)/shard_map/reshape | solution.py:196
  13.5 0.0 copy-done.3
  13.5 0.2 copy.14
  13.7 0.9 %reshape.69.wd_ref = bf16[3,144,144]{2,1,0:T(8,128)(2,1)} reshape(bf16[3,3,48,3,48]{4,3,2,1,0:T(4,128)(2,1)S(1)} %copy.14) | data formatting | bytes 248832 | tf_op jit(solution)/shard_map/reshape | solution.py:197
  14.6 0.6 %pad_add_fusion.pos_ref = s32[2]{0:T(128)} fusion(s32[1]{0:T(128)} %bitcast.1, s32[1]{0:T(128)} %bitcast), kind=kLoop, calls=%fused_computation.8 | loop fusion | flops 2 | bytes 16 | tf_op jit(solution)/shard_map/stack | solution.py:189
  15.2 3.1 %all-to-all-done = bf16[32,16,96]{2,1,0:T(8,128)(2,1)S(1)} async-done(((bf16[32,16,96]{2,1,0:T(8,128)(2,1)}), bf16[32,16,96]{2,1,0:T(8,128)(2,1)S(1)}, u32[]{:S(2)}, u32[]{:S(2)}) %all-to-all-start) | async-done | bytes 98336 | tf_op jit(solution)/shard_map/all_to_all | solution.py:181
  18.3 0.0 copy-start.1
  18.3 0.6 %copy-done.1 = bf16[32,16,96]{2,1,0:T(8,128)(2,1)} copy-done((bf16[32,16,96]{2,1,0:T(8,128)(2,1)}, bf16[32,16,96]{2,1,0:T(8,128)(2,1)S(1)}, u32[]{:S(2)}) %copy-start.1) | copy-done | bytes 98328
  19.0 17.7 %trunk.1 = bf16[48,64,128]{2,1,0:T(8,128)(2,1)} custom-call(s32[2]{0:T(128)} %pad_add_fusion.pos_ref, bf16[512,96]{1,0:T(8,128)(2,1)} %bitcast.17, bf16[144,288]{1,0:T(8,128)(2,1)} %reshape.68.w1_ref, bf16[3,144,144]{2,1,0:T(8,128)(2,1)} %reshape.69.wd_ref, bf16[3,48,48]{2,1,0:T(8,128)(2,1)} %wm_ref.1, f32[48,1]{1,0:T(8,128)} %copy.15.bias_ref, ...), custom_call_target="tpu_custom_call" | custom-call | tf_op jit(solution)/shard_map/trunk/pallas_call | solution.py:147
  (3 shorter events, 0.0 us)
Async XLA Ops:
  0.0 0.9 %copy-start = (bf16[1536,48]{0,1:T(8,128)(2,1)S(1)}, bf16[1536,48]{0,1:T(8,128)(2,1)}, u32[]{:S(2)}) copy-start(bf16[1536,48]{0,1:T(8,128)(2,1)} %param.8) | copy-start | bytes 442372
  0.0 1.8 %copy-start.4 = (bf16[16,1536]{1,0:T(8,128)(2,1)S(1)}, bf16[16,1536]{1,0:T(8,128)(2,1)}, u32[]{:S(2)}) copy-start(bf16[16,1536]{1,0:T(8,128)(2,1)} %param.7) | copy-start | bytes 147460
  0.0 1.8 %copy-start.5 = (bf16[1536,48]{0,1:T(8,128)(2,1)S(1)}, bf16[1536,48]{0,1:T(8,128)(2,1)}, u32[]{:S(2)}) copy-start(bf16[1536,48]{0,1:T(8,128)(2,1)} %param.9) | copy-start | bytes 442372
  2.8 15.5 %all-to-all-start = ((bf16[32,16,96]{2,1,0:T(8,128)(2,1)}), bf16[32,16,96]{2,1,0:T(8,128)(2,1)S(1)}, u32[]{:S(2)}, u32[]{:S(2)}) async-start(bf16[32,16,96]{2,1,0:T(8,128)(2,1)} %broadcast_in_dim.19), calls=%async_computation | async-start | bytes 262144 | tf_op jit(solution)/shard_map/all_to_all | solution.py:181
  10.1 0.7 %copy-start.6 = (f32[48]{0:T(128)S(1)}, f32[48]{0:T(128)}, u32[]{:S(2)}) copy-start(f32[48]{0:T(128)} %param.11) | copy-start | bytes 580
  11.5 0.9 %copy-start.2 = (bf16[3,3,48,48]{3,2,1,0:T(8,128)(2,1)S(1)}, bf16[3,3,48,48]{3,2,1,0:T(8,128)(2,1)}, u32[]{:S(2)}) copy-start(bf16[3,3,48,48]{3,2,1,0:T(8,128)(2,1)} %param.10) | copy-start | bytes 124420
  12.5 1.0 %copy-start.3 = (bf16[3,3,3,48,48]{4,3,2,1,0:T(8,128)(2,1)S(1)}, bf16[3,3,3,48,48]{4,3,2,1,0:T(8,128)(2,1)}, u32[]{:S(2)}) copy-start(bf16[3,3,3,48,48]{4,3,2,1,0:T(8,128)(2,1)} %param.12) | copy-start | bytes 373252
  18.3 0.6 %copy-start.1 = (bf16[32,16,96]{2,1,0:T(8,128)(2,1)}, bf16[32,16,96]{2,1,0:T(8,128)(2,1)S(1)}, u32[]{:S(2)}) copy-start(bf16[32,16,96]{2,1,0:T(8,128)(2,1)S(1)} %all-to-all-done) | copy-start | bytes 294916

commit v2 on v1

v2 whole, which is shorter than its diff:
```python
import functools

import jax
import jax.numpy as jnp
from jax import lax
from jax.experimental import pallas as pl
from jax.experimental.pallas import tpu as pltpu
from jax.sharding import PartitionSpec as P

MARGIN = 16
GROUP = 16
LANES = 128
FAR = -1e30
SPREADS = (2, 4, 8)


def haloed(p_ref, start, count, bins):
    before = pl.multiple_of(jnp.maximum(start - MARGIN, 0), MARGIN)
    after = pl.multiple_of(jnp.minimum(start + count, bins - MARGIN), MARGIN)
    top = p_ref[pl.ds(before, MARGIN), :].astype(jnp.float32)
    mid = p_ref[pl.ds(pl.multiple_of(start, MARGIN), count), :].astype(jnp.float32)
    low = p_ref[pl.ds(after, MARGIN), :].astype(jnp.float32)
    top = jnp.where(start > 0, top, FAR)
    low = jnp.where(start + count < bins, low, FAR)
    return jnp.concatenate([top, mid, low], axis=0)


def trunk(
    rows_tile, cols_tile, bins, channels,
    pos_ref, p_ref, w1_ref, wd_ref, wm_ref, bias_ref, hi_ref, out_ref,
):
    height, width = rows_tile + 2 * MARGIN, cols_tile + 2 * MARGIN
    lanes = height * width
    both = 2 * channels
    z_shape = pltpu.VMEM((3 * channels, GROUP * width), jnp.float32)
    pl.run_scoped(
        functools.partial(
            staged, rows_tile, cols_tile, bins, channels,
            pos_ref, p_ref, w1_ref, wd_ref, wm_ref, bias_ref, hi_ref, out_ref,
        ),
        pltpu.VMEM((height + 2, both, LANES), jnp.bfloat16),
        pltpu.VMEM((both, 4 * width), jnp.bfloat16),
        pltpu.VMEM((channels, lanes), jnp.float32),
        pltpu.VMEM((channels, lanes), jnp.bfloat16),
        pltpu.VMEM((channels, lanes), jnp.bfloat16),
        pltpu.VMEM((channels, lanes), jnp.bfloat16),
        pltpu.VMEM((channels, LANES), jnp.bfloat16),
        pltpu.VMEM((channels * GROUP, LANES), jnp.float32),
        z_shape,
        z_shape,
    )


def staged(
    rows_tile, cols_tile, bins, channels,
    pos_ref, p_ref, w1_ref, wd_ref, wm_ref, bias_ref, hi_ref, out_ref,
    rb, cpat, state, act_a, act_b, side, tail, oscr, z_a, z_b,
):
    width = cols_tile + 2 * MARGIN
    height = rows_tile + 2 * MARGIN
    period = 4 * width
    tiles = period // LANES
    both = 2 * channels
    zero = jnp.bfloat16(0)
    rows_t = jnp.transpose(haloed(p_ref, pos_ref[0], rows_tile, bins)).astype(jnp.bfloat16)
    cols_t = jnp.transpose(haloed(p_ref, pos_ref[1], cols_tile, bins))
    rb[0] = jnp.zeros((both, LANES), jnp.bfloat16)
    rb[height + 1] = jnp.zeros((both, LANES), jnp.bfloat16)
    for i in range(height):
        rb[i + 1] = jnp.broadcast_to(rows_t[:, i : i + 1], (both, LANES))
    cols_s = jnp.concatenate([cols_t[channels:], cols_t[:channels]], axis=0)
    cpat[...] = jnp.concatenate([cols_s] * 4, axis=1).astype(jnp.bfloat16)
    tail[...] = jnp.zeros_like(tail)

    lane = lax.broadcasted_iota(jnp.int32, (both, LANES), 1)

    def at(row0, rows, shift=0):
        start = row0 * width + shift
        return pl.ds(start if isinstance(start, int) else pl.multiple_of(start, LANES), rows * width)

    def gathered(z_ref, rows, spread):
        size = rows * width
        return (
            z_ref[channels : 2 * channels, :size]
            + pltpu.roll(z_ref[:channels, :size], spread, axis=1)
            + pltpu.roll(z_ref[2 * channels :, :size], size - spread, axis=1)
        )

    def grid_part(row0, rows, z_ref):
        size = rows * width
        for pair in range(size // (2 * LANES)):
            halves = []
            for t in (2 * pair, 2 * pair + 1):
                base = 4 * (t // tiles)
                t = t % tiles
                r0 = (t * LANES) // width
                r1 = (t * LANES + LANES - 1) // width
                split = r1 * width - t * LANES
                col = cpat[:, t * LANES : (t + 1) * LANES]
                pieces = []
                for p in (-1, 0, 1):
                    row = rb[row0 + (base + r0 + p + 1)]
                    if r1 != r0:
                        row = jnp.where(lane < split, row, rb[row0 + (base + r1 + p + 1)])
                    pieces.append(jnp.maximum(row + col, zero))
                halves.append(jnp.concatenate(pieces, axis=0))
            x = jnp.concatenate(halves, axis=1)
            z_ref[:, pair * 2 * LANES : (pair + 1) * 2 * LANES] = jnp.dot(
                w1_ref[...], x, preferred_element_type=jnp.float32
            )

    def start_part(row0, rows, z_ref):
        size = rows * width
        st = jnp.minimum(gathered(z_ref, rows, 1) + bias_ref[...], hi_ref[:, at(row0, rows)])
        act = jnp.maximum(st.astype(jnp.bfloat16), zero)
        window = jnp.concatenate([tail[...], act], axis=1)
        tail[...] = act[:, size - LANES :]
        state[:, at(row0, rows)] = st
        act_a[:, at(row0, rows)] = act
        side[:, at(row0, rows)] = window[:, LANES // 2 : LANES // 2 + size]

    stages = [(0, height, grid_part, start_part)]
    src, dst = act_a, act_b
    for block, spread in enumerate(SPREADS):
        shift = spread * width
        ragged = shift % LANES
        assert ragged in (0, LANES // 2)
        edge = 4 if spread == 2 else 2 * spread
        last = block == len(SPREADS) - 1
        around = side if ragged else src

        def conv_part(row0, rows, z_ref, block=block, shift=shift, ragged=ragged, src=src, around=around):
            x = jnp.concatenate(
                [
                    around[:, at(row0, rows, ragged - shift)],
                    src[:, at(row0, rows)],
                    around[:, at(row0, rows, ragged + shift)],
                ],
                axis=0,
            )
            z_ref[:, : rows * width] = jnp.dot(wd_ref[block], x, preferred_element_type=jnp.float32)

        def mix_part(row0, rows, z_ref, block=block, spread=spread, dst=dst, last=last):
            gated = jnp.maximum(gathered(z_ref, rows, spread).astype(jnp.bfloat16), zero)
            st = state[:, at(row0, rows)] + jnp.dot(wm_ref[block], gated, preferred_element_type=jnp.float32)
            if not last:
                state[:, at(row0, rows)] = st
                dst[:, at(row0, rows)] = jnp.maximum(st.astype(jnp.bfloat16), zero)
                return
            for k in range(rows):
                oscr[pl.ds(k, channels, stride=GROUP), :] = st[:, k * width + MARGIN : k * width + MARGIN + LANES]
            start = row0 - MARGIN
            place = pl.ds(start if isinstance(start, int) else pl.multiple_of(start, GROUP), GROUP)
            out_ref[:, place, :] = oscr[...].reshape(channels, GROUP, LANES).astype(jnp.bfloat16)

        stages.append((edge, height - 2 * edge, conv_part, mix_part))
        src, dst = dst, src

    slots = (z_a, z_b)
    waiting = None
    turn = 0
    for first_row, count, before, after in stages:
        groups = count // GROUP
        before(first_row, GROUP, slots[turn])
        if waiting is not None:
            waiting()

        def body(h, carry, first_row=first_row, before=before, after=after, turn=turn):
            row0 = first_row + h * (2 * GROUP)
            before(row0 + GROUP, GROUP, slots[1 - turn])
            after(row0, GROUP, slots[turn])
            before(row0 + 2 * GROUP, GROUP, slots[turn])
            after(row0 + GROUP, GROUP, slots[1 - turn])
            return carry

        lax.fori_loop(0, (groups - 1) // 2, body, 0)
        row0 = first_row + (groups - 1) // 2 * (2 * GROUP)
        sizes = [GROUP] * ((groups - 1) % 2) + [count % GROUP] * (count % GROUP > 0)
        size = GROUP
        for following in sizes:
            before(row0 + size, following, slots[1 - turn])
            after(row0, size, slots[turn])
            row0, size, turn = row0 + size, following, 1 - turn
        waiting = functools.partial(after, row0, size, slots[turn])
        turn = 1 - turn
    waiting()


def call_trunk(rows_tile, cols_tile, bins, channels, *operands):
    vmem = pl.BlockSpec(memory_space=pltpu.VMEM)
    return pl.pallas_call(
        functools.partial(trunk, rows_tile, cols_tile, bins, channels),
        out_shape=jax.ShapeDtypeStruct((channels, rows_tile, cols_tile), jnp.bfloat16),
        in_specs=[pl.BlockSpec(memory_space=pltpu.SMEM)] + [vmem] * 6,
        out_specs=vmem,
        compiler_params=pltpu.CompilerParams(vmem_limit_bytes=56 << 20),
        name="trunk",
    )(*operands)


def local(
    features, first_weight, second_weight, conv_kernel, conv_bias, dilated_kernels, mixing_weights
):
    channels = first_weight.shape[1]
    row_count, col_count = lax.axis_size("row"), lax.axis_size("col")
    devices = row_count * col_count
    mine = jnp.concatenate(
        [
            jnp.dot(features, first_weight, preferred_element_type=jnp.float32),
            jnp.dot(features, second_weight, preferred_element_type=jnp.float32),
        ],
        1,
    ).astype(jnp.bfloat16)
    bins = features.shape[0] * devices
    both = lax.all_to_all(
        jnp.broadcast_to(mine[None], (devices,) + mine.shape), ("row", "col"), 0, 0
    ).reshape(bins, 2 * channels)
    rows_tile = bins // row_count
    cols_tile = bins // col_count
    height, width = rows_tile + 2 * MARGIN, cols_tile + 2 * MARGIN
    row_start = lax.axis_index("row") * rows_tile
    col_start = lax.axis_index("col") * cols_tile
    pos = jnp.stack([row_start, col_start]).astype(jnp.int32)
    row_ids = row_start - MARGIN + jnp.arange(height, dtype=jnp.int32)
    col_ids = col_start - MARGIN + jnp.arange(width, dtype=jnp.int32)
    inside = ((row_ids >= 0) & (row_ids < bins))[:, None] & ((col_ids >= 0) & (col_ids < bins))[None]
    hi = jnp.where(inside, jnp.inf, FAR).astype(jnp.float32).reshape(1, height * width)
    straight = jnp.transpose(conv_kernel, (1, 2, 0, 3))
    swapped = jnp.transpose(conv_kernel, (0, 2, 1, 3))
    w1 = (0.5 * jnp.stack([straight, swapped], axis=3)).astype(jnp.bfloat16).reshape(3 * channels, 6 * channels)
    wd = jnp.transpose(dilated_kernels, (0, 2, 3, 1, 4)).reshape(3, 3 * channels, 3 * channels)
    return call_trunk(
        rows_tile, cols_tile, bins, channels, pos, both, w1, wd, mixing_weights, conv_bias[:, None], hi
    )


def solution(mesh):
    in_specs = (P(("groups", "row", "col"), None), P(), P(), P(), P(), P(), P())
    out_specs = P("groups", "row", "col")
    return jax.shard_map(local, mesh=mesh, in_specs=in_specs, out_specs=out_specs, check_vma=False)
```

time: 36.9 us -> 32.6 us (0.88)
  Pallas kernels: 17.7 us -> 13.4 us
    pallas_call x1, Pallas kernels: 17.7 us -> 13.4 us  [call_trunk(): pl.pallas_call(functools.partial(trunk, rows_tile, cols_tile, bins, chann...]
    mul x0 -> x2, local copies, waits for them, and re-layouts: none -> 0.99 us  [local(): 0.5 * jnp.stack([straight, swapped], axis=3)]
    reshape x1 -> x0, local copies, waits for them, and re-layouts: 0.82 us -> none  [local(): jnp.stack([straight, swapped], axis=3).reshape(3 * channels, 6 * channels)]
  transfers between devices with their start and end apart: 1 -> 1, of which waited for: 1 -> 1; matrix products, arithmetic and copies ran while one was open for 12% -> 13% of each run, Pallas kernels for 0% -> 0%
where the time goes in v2:
time: 32.6 us; the launch traced here: 32.3 us
  Pallas kernels  13.4 us (41%)
  starting transfers between devices  7.3 us (22%)
  local copies, waits for them, and re-layouts  6.51 us (20%)
  waiting for transfers between devices  3.12 us (10%)
  matrix products  1.09 us (3%)
  other arithmetic  0.87 us (3%)
    pallas_call x1, Pallas kernels, call_trunk(): pl.pallas_call(functools.partial(trunk, rows_tile, cols_tile, bins, chann...  13.4 us
    all_to_all x1, starting transfers between devices, local(): lax.all_to_all(jnp.broadcast_to(mine[None], (devices,) + mine.shape), ('r...  7.3 us
    all_to_all x1, waiting for transfers between devices, local(): lax.all_to_all(jnp.broadcast_to(mine[None], (devices,) + mine.shape), ('r...  3.12 us
    unnamed x15, local copies, waits for them, and re-layouts  2.28 us
    mul x2, local copies, waits for them, and re-layouts, local(): 0.5 * jnp.stack([straight, swapped], axis=3)  0.99 us
    dot_general x1, matrix products, local(): jnp.dot(features, first_weight, preferred_element_type=jnp.float32)  0.93 us
    reshape x1, local copies, waits for them, and re-layouts, local(): jnp.transpose(dilated_kernels, (0, 2, 3, 1, 4))  0.93 us
    select_n x1, local copies, waits for them, and re-layouts, local(): jnp.where(inside, jnp.inf, FAR).astype(jnp.float32)  0.76 us
  transfers between devices with their start and end apart: 1, of which 1 were waited for; matrix products, arithmetic and copies ran while one was open for 13% of the time, Pallas kernels for 0%

profile of v2, /device:TPU:0, one launch (start us, length us, event | category | flops | bytes accessed | tf_op | source)
XLA Modules:
  0.0 32.3 jit_solution(10809175300082239695)
XLA Ops:
  0.0 0.0 copy-start
  0.0 0.0 copy-start.4
  0.0 0.0 copy-start.5
  0.0 0.9 %copy-done = bf16[1536,48]{0,1:T(8,128)(2,1)S(1)} copy-done((bf16[1536,48]{0,1:T(8,128)(2,1)S(1)}, bf16[1536,48]{0,1:T(8,128)(2,1)}, u32[]{:S(2)}) %copy-start) | copy-done | bytes 147480
  0.9 0.9 %convolution_convert_fusion.1 = bf16[16,48]{1,0:T(8,128)(2,1)S(1)} fusion(bf16[16,1536]{1,0:T(8,128)(2,1)} %param.7, bf16[1536,48]{0,1:T(8,128)(2,1)S(1)} %copy-done), kind=kOutput, calls=%fused_computation.1 | convolution fusion | flops 2360064 | bytes 198144 | tf_op jit(solution)/shard_map/dot_general | solution.py:209
  1.8 0.0 copy-done.4
  1.8 0.0 copy-done.5
  1.8 0.2 convolution_convert_fusion
  2.0 0.1 pad_maximum_fusion
  2.1 0.7 %broadcast_in_dim.19 = bf16[32,16,96]{2,1,0:T(8,128)(2,1)} broadcast(bf16[16,96]{1,0:T(8,128)(2,1)S(1)} %pad_maximum_fusion), dimensions={1,2} | broadcast | bytes 101376 | tf_op jit(solution)/shard_map/broadcast_in_dim | solution.py:216
  2.8 7.3 %all-to-all-start = ((bf16[32,16,96]{2,1,0:T(8,128)(2,1)}), bf16[32,16,96]{2,1,0:T(8,128)(2,1)S(1)}, u32[]{:S(2)}, u32[]{:S(2)}) async-start(bf16[32,16,96]{2,1,0:T(8,128)(2,1)} %broadcast_in_dim.19), calls=%async_computation | async-start | bytes 262144 | tf_op jit(solution)/shard_map/all_to_all | solution.py:215
  10.1 0.0 copy-start.6
  10.1 0.6 %copy-done.6 = f32[48]{0:T(128)S(1)} copy-done((f32[48]{0:T(128)S(1)}, f32[48]{0:T(128)}, u32[]{:S(2)}) %copy-start.6) | copy-done | bytes 216
  10.8 0.7 %copy.15.bias_ref = f32[48,1]{1,0:T(8,128)} copy(f32[48,1]{0,1:T(1,128)S(1)} %bitcast.21) | data formatting | bytes 384 | tf_op jit(solution)/shard_map/broadcast_in_dim | solution.py:233
  11.5 0.0 copy-start.2
  11.5 0.1 and_select_fusion
  11.6 0.8 %select_n.15.hi_ref = f32[1,15360]{1,0:T(1,128)} reshape(f32[96,160]{1,0:T(8,128)S(1)} %and_select_fusion) | data formatting | bytes 122880 | tf_op jit(solution)/shard_map/jit(_where)/select_n | solution.py:227
  12.3 0.0 copy-done.2
  12.4 0.1 maximum_multiply_fusion
  12.5 0.0 copy-start.3
  12.5 0.2 copy.13
  12.7 0.8 %mul.20.w1_ref = bf16[144,288]{1,0:T(8,128)(2,1)} reshape(bf16[3,48,3,2,48]{4,3,2,1,0:T(2,128)(2,1)S(1)} %copy.13) | data formatting | bytes 165888 | tf_op jit(solution)/shard_map/mul | solution.py:230
  13.5 0.0 copy-done.3
  13.5 0.2 copy.14
  13.7 0.9 %reshape.69.wd_ref = bf16[3,144,144]{2,1,0:T(8,128)(2,1)} reshape(bf16[3,3,48,3,48]{4,3,2,1,0:T(4,128)(2,1)S(1)} %copy.14) | data formatting | bytes 248832 | tf_op jit(solution)/shard_map/reshape | solution.py:231
  14.6 0.6 %pad_add_fusion.pos_ref = s32[2]{0:T(128)} fusion(s32[1]{0:T(128)} %bitcast.1, s32[1]{0:T(128)} %bitcast), kind=kLoop, calls=%fused_computation.8 | loop fusion | flops 2 | bytes 16 | tf_op jit(solution)/shard_map/stack | solution.py:223
  15.2 3.1 %all-to-all-done = bf16[32,16,96]{2,1,0:T(8,128)(2,1)S(1)} async-done(((bf16[32,16,96]{2,1,0:T(8,128)(2,1)}), bf16[32,16,96]{2,1,0:T(8,128)(2,1)S(1)}, u32[]{:S(2)}, u32[]{:S(2)}) %all-to-all-start) | async-done | bytes 98336 | tf_op jit(solution)/shard_map/all_to_all | solution.py:215
  18.3 0.0 copy-start.1
  18.3 0.6 %copy-done.1 = bf16[32,16,96]{2,1,0:T(8,128)(2,1)} copy-done((bf16[32,16,96]{2,1,0:T(8,128)(2,1)}, bf16[32,16,96]{2,1,0:T(8,128)(2,1)S(1)}, u32[]{:S(2)}) %copy-start.1) | copy-done | bytes 98328
  19.0 13.4 %trunk.1 = bf16[48,64,128]{2,1,0:T(8,128)(2,1)} custom-call(s32[2]{0:T(128)} %pad_add_fusion.pos_ref, bf16[512,96]{1,0:T(8,128)(2,1)} %bitcast.17, bf16[144,288]{1,0:T(8,128)(2,1)} %mul.20.w1_ref, bf16[3,144,144]{2,1,0:T(8,128)(2,1)} %reshape.69.wd_ref, bf16[3,48,48]{2,1,0:T(8,128)(2,1)} %wm_ref.1, f32[48,1]{1,0:T(8,128)} %copy.15.bias_ref, ...), custom_call_target="tpu_custom_call" | custom-call | tf_op jit(solution)/shard_map/trunk/pallas_call | solution.py:191
  (3 shorter events, 0.0 us)
Async XLA Ops:
  0.0 0.9 %copy-start = (bf16[1536,48]{0,1:T(8,128)(2,1)S(1)}, bf16[1536,48]{0,1:T(8,128)(2,1)}, u32[]{:S(2)}) copy-start(bf16[1536,48]{0,1:T(8,128)(2,1)} %param.8) | copy-start | bytes 442372
  0.0 1.8 %copy-start.4 = (bf16[16,1536]{1,0:T(8,128)(2,1)S(1)}, bf16[16,1536]{1,0:T(8,128)(2,1)}, u32[]{:S(2)}) copy-start(bf16[16,1536]{1,0:T(8,128)(2,1)} %param.7) | copy-start | bytes 147460
  0.0 1.8 %copy-start.5 = (bf16[1536,48]{0,1:T(8,128)(2,1)S(1)}, bf16[1536,48]{0,1:T(8,128)(2,1)}, u32[]{:S(2)}) copy-start(bf16[1536,48]{0,1:T(8,128)(2,1)} %param.9) | copy-start | bytes 442372
  2.8 15.5 %all-to-all-start = ((bf16[32,16,96]{2,1,0:T(8,128)(2,1)}), bf16[32,16,96]{2,1,0:T(8,128)(2,1)S(1)}, u32[]{:S(2)}, u32[]{:S(2)}) async-start(bf16[32,16,96]{2,1,0:T(8,128)(2,1)} %broadcast_in_dim.19), calls=%async_computation | async-start | bytes 262144 | tf_op jit(solution)/shard_map/all_to_all | solution.py:215
  10.1 0.7 %copy-start.6 = (f32[48]{0:T(128)S(1)}, f32[48]{0:T(128)}, u32[]{:S(2)}) copy-start(f32[48]{0:T(128)} %param.11) | copy-start | bytes 580
  11.5 0.9 %copy-start.2 = (bf16[3,3,48,48]{3,2,1,0:T(8,128)(2,1)S(1)}, bf16[3,3,48,48]{3,2,1,0:T(8,128)(2,1)}, u32[]{:S(2)}) copy-start(bf16[3,3,48,48]{3,2,1,0:T(8,128)(2,1)} %param.10) | copy-start | bytes 124420
  12.5 1.0 %copy-start.3 = (bf16[3,3,3,48,48]{4,3,2,1,0:T(8,128)(2,1)S(1)}, bf16[3,3,3,48,48]{4,3,2,1,0:T(8,128)(2,1)}, u32[]{:S(2)}) copy-start(bf16[3,3,3,48,48]{4,3,2,1,0:T(8,128)(2,1)} %param.12) | copy-start | bytes 373252
  18.3 0.6 %copy-start.1 = (bf16[32,16,96]{2,1,0:T(8,128)(2,1)}, bf16[32,16,96]{2,1,0:T(8,128)(2,1)S(1)}, u32[]{:S(2)}) copy-start(bf16[32,16,96]{2,1,0:T(8,128)(2,1)S(1)} %all-to-all-done) | copy-start | bytes 294916

commit v3 on v2

--- a/solution.py
+++ b/solution.py
@@ -186,6 +186,23 @@
     waiting()
 
 
+def project(count, f_ref, first_ref, second_ref, out_ref):
+    weights = jnp.concatenate([first_ref[...], second_ref[...]], axis=0)
+    mine = lax.dot_general(
+        f_ref[...], weights, (((1,), (1,)), ((), ())), preferred_element_type=jnp.float32
+    ).astype(jnp.bfloat16)
+    out_ref[...] = jnp.broadcast_to(mine[None], (count,) + mine.shape)
+
+
+def vmem_need(rows_tile, cols_tile, channels):
+    height, width = rows_tile + 2 * MARGIN, cols_tile + 2 * MARGIN
+    lanes = height * width
+    cells = lanes * channels
+    sums = 2 * 3 * channels * GROUP * width * 4
+    grid = (height + 2) * 2 * channels * LANES * 2
+    return cells * 4 + 3 * cells * 2 + sums + grid + channels * rows_tile * LANES * 2 + (6 << 20)
+
+
 def call_trunk(rows_tile, cols_tile, bins, channels, *operands):
     vmem = pl.BlockSpec(memory_space=pltpu.VMEM)
     return pl.pallas_call(
@@ -193,7 +210,7 @@
         out_shape=jax.ShapeDtypeStruct((channels, rows_tile, cols_tile), jnp.bfloat16),
         in_specs=[pl.BlockSpec(memory_space=pltpu.SMEM)] + [vmem] * 6,
         out_specs=vmem,
-        compiler_params=pltpu.CompilerParams(vmem_limit_bytes=56 << 20),
+        compiler_params=pltpu.CompilerParams(vmem_limit_bytes=vmem_need(rows_tile, cols_tile, channels)),
         name="trunk",
     )(*operands)
 
@@ -204,17 +221,17 @@
     channels = first_weight.shape[1]
     row_count, col_count = lax.axis_size("row"), lax.axis_size("col")
     devices = row_count * col_count
-    mine = jnp.concatenate(
-        [
-            jnp.dot(features, first_weight, preferred_element_type=jnp.float32),
-            jnp.dot(features, second_weight, preferred_element_type=jnp.float32),
-        ],
-        1,
-    ).astype(jnp.bfloat16)
     bins = features.shape[0] * devices
-    both = lax.all_to_all(
-        jnp.broadcast_to(mine[None], (devices,) + mine.shape), ("row", "col"), 0, 0
-    ).reshape(bins, 2 * channels)
+    vmem = pl.BlockSpec(memory_space=pltpu.VMEM)
+    copies = pl.pallas_call(
+        functools.partial(project, devices),
+        out_shape=jax.ShapeDtypeStruct((devices, features.shape[0], 2 * channels), jnp.bfloat16),
+        in_specs=[vmem] * 3,
+        out_specs=vmem,
+        compiler_params=pltpu.CompilerParams(vmem_limit_bytes=60 << 20),
+        name="project",
+    )(features, first_weight.T, second_weight.T)
+    both = lax.all_to_all(copies, ("row", "col"), 0, 0).reshape(bins, 2 * channels)
     rows_tile = bins // row_count
     cols_tile = bins // col_count
     height, width = rows_tile + 2 * MARGIN, cols_tile + 2 * MARGIN

time: 32.6 us -> 30.5 us (0.936)
  local copies, waits for them, and re-layouts: 6.51 us -> 2.92 us
  waiting for transfers between devices: 3.12 us -> 4.98 us
  Pallas kernels: 13.4 us -> 14.7 us
  matrix products: 1.09 us -> 0 us
  other arithmetic: 0.87 us -> 0.23 us
    pallas_call x0 -> x1, Pallas kernels: none -> 1.87 us  [local(): pl.pallas_call(functools.partial(project, devices), out_shape=jax.ShapeDt...]
    all_to_all x1, waiting for transfers between devices: 3.12 us -> 4.98 us  [local(): lax.all_to_all(copies, ('row', 'col'), 0, 0).reshape(bins, 2 * channels)]
    dot_general x2 -> x0, matrix products: 1.09 us -> none  [the longest x1 0.93 us: local(): jnp.dot(features, first_weight, preferred_element_type=jnp.float32)]
    reshape x1, local copies, waits for them, and re-layouts: 0.93 us -> 0.22 us  [local(): jnp.transpose(dilated_kernels, (0, 2, 3, 1, 4))]
    broadcast_in_dim x1 -> x0, local copies, waits for them, and re-layouts: 0.69 us -> none  [local(): jnp.broadcast_to(mine[None], (devices,) + mine.shape)]
    mul x2, local copies, waits for them, and re-layouts: 0.99 us -> 0.34 us  [local(): 0.5 * jnp.stack([straight, swapped], axis=3)]
    select_n x1, local copies, waits for them, and re-layouts: 0.76 us -> 0.14 us  [local(): jnp.where(inside, jnp.inf, FAR).astype(jnp.float32)]
    broadcast_in_dim x1, local copies, waits for them, and re-layouts: 0.7 us -> 0.09 us  [local(): conv_bias[:, None]]
  transfers between devices with their start and end apart: 1 -> 1, of which waited for: 1 -> 1; matrix products, arithmetic and copies ran while one was open for 13% -> 4% of each run, Pallas kernels for 0% -> 0%
where the time goes in v3:
time: 30.5 us; the launch traced here: 30.3 us
  Pallas kernels  14.7 us (48%)
  starting transfers between devices  7.3 us (24%)
  waiting for transfers between devices  4.98 us (16%)
  local copies, waits for them, and re-layouts  2.92 us (10%)
    pallas_call x1, Pallas kernels, call_trunk(): pl.pallas_call(functools.partial(trunk, rows_tile, cols_tile, bins, chann...  12.9 us
    all_to_all x1, starting transfers between devices, local(): lax.all_to_all(copies, ('row', 'col'), 0, 0).reshape(bins, 2 * channels)  7.3 us
    all_to_all x1, waiting for transfers between devices, local(): lax.all_to_all(copies, ('row', 'col'), 0, 0).reshape(bins, 2 * channels)  4.98 us
    unnamed x9, local copies, waits for them, and re-layouts  1.94 us
    pallas_call x1, Pallas kernels, local(): pl.pallas_call(functools.partial(project, devices), out_shape=jax.ShapeDt...  1.87 us
  transfers between devices with their start and end apart: 1, of which 1 were waited for; matrix products, arithmetic and copies ran while one was open for 4% of the time, Pallas kernels for 0%

profile of v3, /device:TPU:0, one launch (start us, length us, event | category | flops | bytes accessed | tf_op | source)
XLA Modules:
  0.0 30.3 jit_solution(7984856683187392492)
XLA Ops:
  0.0 1.9 %project.1 = bf16[32,16,96]{2,1,0:T(8,128)(2,1)} custom-call(bf16[16,1536]{1,0:T(8,128)(2,1)} %f_ref.1, bf16[48,1536]{1,0:T(8,128)(2,1)} %bitcast.19, bf16[48,1536]{1,0:T(8,128)(2,1)} %bitcast.20), custom_call_target="tpu_custom_call" | custom-call | tf_op jit(solution)/shard_map/project/pallas_call | solution.py:226
  1.9 7.3 %all-to-all-start = ((bf16[32,16,96]{2,1,0:T(8,128)(2,1)}), bf16[32,16,96]{2,1,0:T(8,128)(2,1)S(1)}, u32[]{:S(2)}, u32[]{:S(2)}) async-start(bf16[32,16,96]{2,1,0:T(8,128)(2,1)} %project.1), calls=%async_computation | async-start | bytes 262144 | tf_op jit(solution)/shard_map/all_to_all | solution.py:234
  9.2 0.0 copy-start.3
  9.2 0.6 %copy-done.3 = f32[48]{0:T(128)S(1)} copy-done((f32[48]{0:T(128)S(1)}, f32[48]{0:T(128)}, u32[]{:S(2)}) %copy-start.3) | copy-done | bytes 216
  9.9 0.1 copy.15.bias_ref
  10.0 0.0 copy-start.1
  10.0 0.1 and_select_fusion
  10.0 0.1 select_n.15.hi_ref
  10.2 0.7 %copy-done.1 = bf16[3,3,48,48]{3,2,1,0:T(8,128)(2,1)S(1)} copy-done((bf16[3,3,48,48]{3,2,1,0:T(8,128)(2,1)S(1)}, bf16[3,3,48,48]{3,2,1,0:T(8,128)(2,1)}, u32[]{:S(2)}) %copy-start.1) | copy-done | bytes 41496
  10.9 0.1 maximum_multiply_fusion
  10.9 0.0 copy-start.2
  10.9 0.2 copy.13
  11.1 0.2 mul.20.w1_ref
  11.3 0.6 %copy-done.2 = bf16[3,3,3,48,48]{4,3,2,1,0:T(8,128)(2,1)S(1)} copy-done((bf16[3,3,3,48,48]{4,3,2,1,0:T(8,128)(2,1)S(1)}, bf16[3,3,3,48,48]{4,3,2,1,0:T(8,128)(2,1)}, u32[]{:S(2)}) %copy-start.2) | copy-done | bytes 124440
  11.9 0.2 copy.14
  12.1 0.0 copy-start
  12.1 0.2 reshape.54.wd_ref
  12.3 0.1 pad_add_fusion.pos_ref
  12.4 5.0 %all-to-all-done = bf16[32,16,96]{2,1,0:T(8,128)(2,1)S(1)} async-done(((bf16[32,16,96]{2,1,0:T(8,128)(2,1)}), bf16[32,16,96]{2,1,0:T(8,128)(2,1)S(1)}, u32[]{:S(2)}, u32[]{:S(2)}) %all-to-all-start) | async-done | bytes 98336 | tf_op jit(solution)/shard_map/all_to_all | solution.py:234
  17.4 0.0 copy-done
  17.4 12.9 %trunk.1 = bf16[48,64,128]{2,1,0:T(8,128)(2,1)} custom-call(s32[2]{0:T(128)S(1)} %pad_add_fusion.pos_ref, bf16[512,96]{1,0:T(8,128)(2,1)S(1)} %bitcast.15, bf16[144,288]{1,0:T(8,128)(2,1)S(1)} %mul.20.w1_ref, bf16[3,144,144]{2,1,0:T(8,128)(2,1)S(1)} %reshape.54.wd_ref, bf16[3,48,48]{2,1,0:T(8,128)(2,1)S(1)} %copy-done, f32[48,1]{1,0:T(8,128)S(1)} %copy.15.bias_ref, ...), custom_call_target="tpu_custom_call" | custom-call | tf_op jit(solution)/shard_map/trunk/pallas_call | solution.py:208
  (3 shorter events, 0.0 us)
Async XLA Ops:
  1.9 15.5 %all-to-all-start = ((bf16[32,16,96]{2,1,0:T(8,128)(2,1)}), bf16[32,16,96]{2,1,0:T(8,128)(2,1)S(1)}, u32[]{:S(2)}, u32[]{:S(2)}) async-start(bf16[32,16,96]{2,1,0:T(8,128)(2,1)} %project.1), calls=%async_computation | async-start | bytes 262144 | tf_op jit(solution)/shard_map/all_to_all | solution.py:234
  9.2 0.7 %copy-start.3 = (f32[48]{0:T(128)S(1)}, f32[48]{0:T(128)}, u32[]{:S(2)}) copy-start(f32[48]{0:T(128)} %param.11) | copy-start | bytes 580
  10.0 0.9 %copy-start.1 = (bf16[3,3,48,48]{3,2,1,0:T(8,128)(2,1)S(1)}, bf16[3,3,48,48]{3,2,1,0:T(8,128)(2,1)}, u32[]{:S(2)}) copy-start(bf16[3,3,48,48]{3,2,1,0:T(8,128)(2,1)} %param.10) | copy-start | bytes 124420
  10.9 1.0 %copy-start.2 = (bf16[3,3,3,48,48]{4,3,2,1,0:T(8,128)(2,1)S(1)}, bf16[3,3,3,48,48]{4,3,2,1,0:T(8,128)(2,1)}, u32[]{:S(2)}) copy-start(bf16[3,3,3,48,48]{4,3,2,1,0:T(8,128)(2,1)} %param.12) | copy-start | bytes 373252
  12.1 5.3 %copy-start = (bf16[3,48,48]{2,1,0:T(8,128)(2,1)S(1)}, bf16[3,48,48]{2,1,0:T(8,128)(2,1)}, u32[]{:S(2)}) copy-start(bf16[3,48,48]{2,1,0:T(8,128)(2,1)} %wm_ref.1) | copy-start | bytes 41476

commit v4 on v3

--- a/solution.py
+++ b/solution.py
@@ -27,7 +27,7 @@
 
 def trunk(
     rows_tile, cols_tile, bins, channels,
-    pos_ref, p_ref, w1_ref, wd_ref, wm_ref, bias_ref, hi_ref, out_ref,
+    pos_ref, p_ref, w1_ref, wd_ref, wm_ref, bias_ref, hi_ref, out_ref, staging, sems,
 ):
     height, width = rows_tile + 2 * MARGIN, cols_tile + 2 * MARGIN
     lanes = height * width
@@ -36,7 +36,7 @@
     pl.run_scoped(
         functools.partial(
             staged, rows_tile, cols_tile, bins, channels,
-            pos_ref, p_ref, w1_ref, wd_ref, wm_ref, bias_ref, hi_ref, out_ref,
+            pos_ref, p_ref, w1_ref, wd_ref, wm_ref, bias_ref, hi_ref, out_ref, staging, sems,
         ),
         pltpu.VMEM((height + 2, both, LANES), jnp.bfloat16),
         pltpu.VMEM((both, 4 * width), jnp.bfloat16),
@@ -46,6 +46,7 @@
         pltpu.VMEM((channels, lanes), jnp.bfloat16),
         pltpu.VMEM((channels, LANES), jnp.bfloat16),
         pltpu.VMEM((channels * GROUP, LANES), jnp.float32),
+        pltpu.VMEM((channels * GROUP, LANES), jnp.float32),
         z_shape,
         z_shape,
     )
@@ -53,8 +54,8 @@
 
 def staged(
     rows_tile, cols_tile, bins, channels,
-    pos_ref, p_ref, w1_ref, wd_ref, wm_ref, bias_ref, hi_ref, out_ref,
-    rb, cpat, state, act_a, act_b, side, tail, oscr, z_a, z_b,
+    pos_ref, p_ref, w1_ref, wd_ref, wm_ref, bias_ref, hi_ref, out_ref, staging, sems,
+    rb, cpat, state, act_a, act_b, side, tail, flat_a, flat_b, z_a, z_b,
 ):
     width = cols_tile + 2 * MARGIN
     height = rows_tile + 2 * MARGIN
@@ -66,8 +67,14 @@
     cols_t = jnp.transpose(haloed(p_ref, pos_ref[1], cols_tile, bins))
     rb[0] = jnp.zeros((both, LANES), jnp.bfloat16)
     rb[height + 1] = jnp.zeros((both, LANES), jnp.bfloat16)
-    for i in range(height):
-        rb[i + 1] = jnp.broadcast_to(rows_t[:, i : i + 1], (both, LANES))
+    ready = set()
+
+    def prepare(start, stop):
+        for i in range(max(start, 0), min(stop, height)):
+            if i not in ready:
+                ready.add(i)
+                rb[i + 1] = jnp.broadcast_to(rows_t[:, i : i + 1], (both, LANES))
+
     cols_s = jnp.concatenate([cols_t[channels:], cols_t[:channels]], axis=0)
     cpat[...] = jnp.concatenate([cols_s] * 4, axis=1).astype(jnp.bfloat16)
     tail[...] = jnp.zeros_like(tail)
@@ -88,6 +95,8 @@
 
     def grid_part(row0, rows, z_ref):
         size = rows * width
+        if isinstance(row0, int):
+            prepare(row0 - 1, row0 + rows + 1)
         for pair in range(size // (2 * LANES)):
             halves = []
             for t in (2 * pair, 2 * pair + 1):
@@ -143,18 +152,26 @@
         def mix_part(row0, rows, z_ref, block=block, spread=spread, dst=dst, last=last):
             gated = jnp.maximum(gathered(z_ref, rows, spread).astype(jnp.bfloat16), zero)
             st = state[:, at(row0, rows)] + jnp.dot(wm_ref[block], gated, preferred_element_type=jnp.float32)
+            flat = flat_a if z_ref is z_a else flat_b
             if not last:
                 state[:, at(row0, rows)] = st
                 dst[:, at(row0, rows)] = jnp.maximum(st.astype(jnp.bfloat16), zero)
                 return
+            st = st.astype(jnp.bfloat16)
             for k in range(rows):
-                oscr[pl.ds(k, channels, stride=GROUP), :] = st[:, k * width + MARGIN : k * width + MARGIN + LANES]
+                row = st[:, k * width + MARGIN : k * width + MARGIN + LANES]
+                flat[pl.ds(k, channels, stride=GROUP), :] = row.astype(jnp.float32)
             start = row0 - MARGIN
             place = pl.ds(start if isinstance(start, int) else pl.multiple_of(start, GROUP), GROUP)
-            out_ref[:, place, :] = oscr[...].reshape(channels, GROUP, LANES).astype(jnp.bfloat16)
+            staging[:, place, :] = flat[...].reshape(channels, GROUP, LANES).astype(jnp.bfloat16)
+            sent(start).start()
 
         stages.append((edge, height - 2 * edge, conv_part, mix_part))
         src, dst = dst, src
+
+    def sent(start):
+        place = pl.ds(start if isinstance(start, int) else pl.multiple_of(start, GROUP), GROUP)
+        return pltpu.make_async_copy(staging.at[:, place, :], out_ref.at[:, place, :], sems.at[start // GROUP])
 
     slots = (z_a, z_b)
     waiting = None
@@ -173,8 +190,15 @@
             after(row0 + GROUP, GROUP, slots[1 - turn])
             return carry
 
-        lax.fori_loop(0, (groups - 1) // 2, body, 0)
-        row0 = first_row + (groups - 1) // 2 * (2 * GROUP)
+        loops = (groups - 1) // 2
+        if loops > 2:
+            if before is grid_part:
+                prepare(0, height)
+            lax.fori_loop(0, loops, body, 0)
+        else:
+            for h in range(loops):
+                body(h, 0)
+        row0 = first_row + loops * (2 * GROUP)
         sizes = [GROUP] * ((groups - 1) % 2) + [count % GROUP] * (count % GROUP > 0)
         size = GROUP
         for following in sizes:
@@ -184,6 +208,8 @@
         waiting = functools.partial(after, row0, size, slots[turn])
         turn = 1 - turn
     waiting()
+    for start in range(0, rows_tile, GROUP):
+        sent(start).wait()
 
 
 def project(count, f_ref, first_ref, second_ref, out_ref):
@@ -209,7 +235,11 @@
         functools.partial(trunk, rows_tile, cols_tile, bins, channels),
         out_shape=jax.ShapeDtypeStruct((channels, rows_tile, cols_tile), jnp.bfloat16),
         in_specs=[pl.BlockSpec(memory_space=pltpu.SMEM)] + [vmem] * 6,
-        out_specs=vmem,
+        out_specs=pl.BlockSpec(memory_space=pltpu.HBM),
+        scratch_shapes=[
+            pltpu.VMEM((channels, rows_tile, cols_tile), jnp.bfloat16),
+            pltpu.SemaphoreType.DMA((rows_tile // GROUP,)),
+        ],
         compiler_params=pltpu.CompilerParams(vmem_limit_bytes=vmem_need(rows_tile, cols_tile, channels)),
         name="trunk",
     )(*operands)

time: 30.5 us -> 28 us (0.918)
  Pallas kernels: 14.7 us -> 12.2 us
    pallas_call x1, Pallas kernels: 12.9 us -> 10.3 us  [call_trunk(): pl.pallas_call(functools.partial(trunk, rows_tile, cols_tile, bins, chann...]
where the time goes in v4:
time: 28 us; the launch traced here: 27.7 us
  Pallas kernels  12.2 us (44%)
  starting transfers between devices  7.3 us (26%)
  waiting for transfers between devices  4.98 us (18%)
  local copies, waits for them, and re-layouts  2.92 us (10%)
    pallas_call x1, Pallas kernels, call_trunk(): pl.pallas_call(functools.partial(trunk, rows_tile, cols_tile, bins, chann...  10.3 us
    all_to_all x1, starting transfers between devices, local(): lax.all_to_all(copies, ('row', 'col'), 0, 0).reshape(bins, 2 * channels)  7.3 us
    all_to_all x1, waiting for transfers between devices, local(): lax.all_to_all(copies, ('row', 'col'), 0, 0).reshape(bins, 2 * channels)  4.98 us
    unnamed x9, local copies, waits for them, and re-layouts  1.94 us
    pallas_call x1, Pallas kernels, local(): pl.pallas_call(functools.partial(project, devices), out_shape=jax.ShapeDt...  1.87 us
  transfers between devices with their start and end apart: 1, of which 1 were waited for; matrix products, arithmetic and copies ran while one was open for 4% of the time, Pallas kernels for 0%

profile of v4, /device:TPU:0, one launch (start us, length us, event | category | flops | bytes accessed | tf_op | source)
XLA Modules:
  0.0 27.7 jit_solution(17685502978772604848)
XLA Ops:
  0.0 1.9 %project.1 = bf16[32,16,96]{2,1,0:T(8,128)(2,1)} custom-call(bf16[16,1536]{1,0:T(8,128)(2,1)} %f_ref.1, bf16[48,1536]{1,0:T(8,128)(2,1)} %bitcast.19, bf16[48,1536]{1,0:T(8,128)(2,1)} %bitcast.20), custom_call_target="tpu_custom_call" | custom-call | tf_op jit(solution)/shard_map/project/pallas_call | solution.py:256
  1.9 7.3 %all-to-all-start = ((bf16[32,16,96]{2,1,0:T(8,128)(2,1)}), bf16[32,16,96]{2,1,0:T(8,128)(2,1)S(1)}, u32[]{:S(2)}, u32[]{:S(2)}) async-start(bf16[32,16,96]{2,1,0:T(8,128)(2,1)} %project.1), calls=%async_computation | async-start | bytes 262144 | tf_op jit(solution)/shard_map/all_to_all | solution.py:264
  9.2 0.0 copy-start.3
  9.2 0.6 %copy-done.3 = f32[48]{0:T(128)S(1)} copy-done((f32[48]{0:T(128)S(1)}, f32[48]{0:T(128)}, u32[]{:S(2)}) %copy-start.3) | copy-done | bytes 216
  9.9 0.1 copy.15.bias_ref
  10.0 0.0 copy-start.1
  10.0 0.1 and_select_fusion
  10.0 0.1 select_n.15.hi_ref
  10.2 0.7 %copy-done.1 = bf16[3,3,48,48]{3,2,1,0:T(8,128)(2,1)S(1)} copy-done((bf16[3,3,48,48]{3,2,1,0:T(8,128)(2,1)S(1)}, bf16[3,3,48,48]{3,2,1,0:T(8,128)(2,1)}, u32[]{:S(2)}) %copy-start.1) | copy-done | bytes 41496
  10.9 0.1 maximum_multiply_fusion
  10.9 0.0 copy-start.2
  10.9 0.2 copy.13
  11.1 0.2 mul.20.w1_ref
  11.3 0.6 %copy-done.2 = bf16[3,3,3,48,48]{4,3,2,1,0:T(8,128)(2,1)S(1)} copy-done((bf16[3,3,3,48,48]{4,3,2,1,0:T(8,128)(2,1)S(1)}, bf16[3,3,3,48,48]{4,3,2,1,0:T(8,128)(2,1)}, u32[]{:S(2)}) %copy-start.2) | copy-done | bytes 124440
  11.9 0.2 copy.14
  12.1 0.0 copy-start
  12.1 0.2 reshape.54.wd_ref
  12.3 0.1 pad_add_fusion.pos_ref
  12.4 5.0 %all-to-all-done = bf16[32,16,96]{2,1,0:T(8,128)(2,1)S(1)} async-done(((bf16[32,16,96]{2,1,0:T(8,128)(2,1)}), bf16[32,16,96]{2,1,0:T(8,128)(2,1)S(1)}, u32[]{:S(2)}, u32[]{:S(2)}) %all-to-all-start) | async-done | bytes 98336 | tf_op jit(solution)/shard_map/all_to_all | solution.py:264
  17.4 0.0 copy-done
  17.4 10.3 %trunk.1 = bf16[48,64,128]{2,1,0:T(8,128)(2,1)} custom-call(s32[2]{0:T(128)S(1)} %pad_add_fusion.pos_ref, bf16[512,96]{1,0:T(8,128)(2,1)S(1)} %bitcast.15, bf16[144,288]{1,0:T(8,128)(2,1)S(1)} %mul.20.w1_ref, bf16[3,144,144]{2,1,0:T(8,128)(2,1)S(1)} %reshape.54.wd_ref, bf16[3,48,48]{2,1,0:T(8,128)(2,1)S(1)} %copy-done, f32[48,1]{1,0:T(8,128)S(1)} %copy.15.bias_ref, ...), custom_call_target="tpu_custom_call" | custom-call | tf_op jit(solution)/shard_map/trunk/pallas_call | solution.py:234
  (3 shorter events, 0.0 us)
Async XLA Ops:
  1.9 15.5 %all-to-all-start = ((bf16[32,16,96]{2,1,0:T(8,128)(2,1)}), bf16[32,16,96]{2,1,0:T(8,128)(2,1)S(1)}, u32[]{:S(2)}, u32[]{:S(2)}) async-start(bf16[32,16,96]{2,1,0:T(8,128)(2,1)} %project.1), calls=%async_computation | async-start | bytes 262144 | tf_op jit(solution)/shard_map/all_to_all | solution.py:264
  9.2 0.7 %copy-start.3 = (f32[48]{0:T(128)S(1)}, f32[48]{0:T(128)}, u32[]{:S(2)}) copy-start(f32[48]{0:T(128)} %param.11) | copy-start | bytes 580
  10.0 0.9 %copy-start.1 = (bf16[3,3,48,48]{3,2,1,0:T(8,128)(2,1)S(1)}, bf16[3,3,48,48]{3,2,1,0:T(8,128)(2,1)}, u32[]{:S(2)}) copy-start(bf16[3,3,48,48]{3,2,1,0:T(8,128)(2,1)} %param.10) | copy-start | bytes 124420
  10.9 1.0 %copy-start.2 = (bf16[3,3,3,48,48]{4,3,2,1,0:T(8,128)(2,1)S(1)}, bf16[3,3,3,48,48]{4,3,2,1,0:T(8,128)(2,1)}, u32[]{:S(2)}) copy-start(bf16[3,3,3,48,48]{4,3,2,1,0:T(8,128)(2,1)} %param.12) | copy-start | bytes 373252
  12.1 5.3 %copy-start = (bf16[3,48,48]{2,1,0:T(8,128)(2,1)S(1)}, bf16[3,48,48]{2,1,0:T(8,128)(2,1)}, u32[]{:S(2)}) copy-start(bf16[3,48,48]{2,1,0:T(8,128)(2,1)} %wm_ref.1) | copy-start | bytes 41476

commit v5 on v4

--- a/solution.py
+++ b/solution.py
@@ -9,6 +9,7 @@
 
 MARGIN = 16
 GROUP = 16
+PITCH = GROUP + 1
 LANES = 128
 FAR = -1e30
 SPREADS = (2, 4, 8)
@@ -45,8 +46,8 @@
         pltpu.VMEM((channels, lanes), jnp.bfloat16),
         pltpu.VMEM((channels, lanes), jnp.bfloat16),
         pltpu.VMEM((channels, LANES), jnp.bfloat16),
-        pltpu.VMEM((channels * GROUP, LANES), jnp.float32),
-        pltpu.VMEM((channels * GROUP, LANES), jnp.float32),
+        pltpu.VMEM((channels * PITCH, LANES), jnp.float32),
+        pltpu.VMEM((channels * PITCH, LANES), jnp.float32),
         z_shape,
         z_shape,
     )
@@ -128,6 +129,12 @@
         act_a[:, at(row0, rows)] = act
         side[:, at(row0, rows)] = window[:, LANES // 2 : LANES // 2 + size]
 
+    pending = []
+
+    def flush():
+        while pending:
+            pending.pop()()
+
     stages = [(0, height, grid_part, start_part)]
     src, dst = act_a, act_b
     for block, spread in enumerate(SPREADS):
@@ -151,20 +158,27 @@
 
         def mix_part(row0, rows, z_ref, block=block, spread=spread, dst=dst, last=last):
             gated = jnp.maximum(gathered(z_ref, rows, spread).astype(jnp.bfloat16), zero)
+            if last:
+                flush()
             st = state[:, at(row0, rows)] + jnp.dot(wm_ref[block], gated, preferred_element_type=jnp.float32)
             flat = flat_a if z_ref is z_a else flat_b
             if not last:
                 state[:, at(row0, rows)] = st
                 dst[:, at(row0, rows)] = jnp.maximum(st.astype(jnp.bfloat16), zero)
-                return
-            st = st.astype(jnp.bfloat16)
-            for k in range(rows):
-                row = st[:, k * width + MARGIN : k * width + MARGIN + LANES]
-                flat[pl.ds(k, channels, stride=GROUP), :] = row.astype(jnp.float32)
-            start = row0 - MARGIN
-            place = pl.ds(start if isinstance(start, int) else pl.multiple_of(start, GROUP), GROUP)
-            staging[:, place, :] = flat[...].reshape(channels, GROUP, LANES).astype(jnp.bfloat16)
-            sent(start).start()
+                return None
+            result = st.astype(jnp.bfloat16)
+
+            def send():
+                for k in range(rows):
+                    row = result[:, k * width + MARGIN : k * width + MARGIN + LANES]
+                    flat[pl.ds(k, channels, stride=PITCH), :] = row.astype(jnp.float32)
+                start = row0 - MARGIN
+                place = pl.ds(start if isinstance(start, int) else pl.multiple_of(start, GROUP), GROUP)
+                for c in range(channels):
+                    staging[c, place, :] = flat[c * PITCH : c * PITCH + GROUP, :].astype(jnp.bfloat16)
+                sent(start).start()
+
+            return send
 
         stages.append((edge, height - 2 * edge, conv_part, mix_part))
         src, dst = dst, src
@@ -174,6 +188,11 @@
         return pltpu.make_async_copy(staging.at[:, place, :], out_ref.at[:, place, :], sems.at[start // GROUP])
 
     slots = (z_a, z_b)
+    def run(after, *place):
+        send = after(*place)
+        if send is not None:
+            pending.append(send)
+
     waiting = None
     turn = 0
     for first_row, count, before, after in stages:
@@ -185,16 +204,22 @@
         def body(h, carry, first_row=first_row, before=before, after=after, turn=turn):
             row0 = first_row + h * (2 * GROUP)
             before(row0 + GROUP, GROUP, slots[1 - turn])
-            after(row0, GROUP, slots[turn])
+            run(after, row0, GROUP, slots[turn])
             before(row0 + 2 * GROUP, GROUP, slots[turn])
-            after(row0 + GROUP, GROUP, slots[1 - turn])
+            run(after, row0 + GROUP, GROUP, slots[1 - turn])
             return carry
 
         loops = (groups - 1) // 2
         if loops > 2:
             if before is grid_part:
                 prepare(0, height)
-            lax.fori_loop(0, loops, body, 0)
+
+            def closed(h, carry, body=body):
+                body(h, carry)
+                flush()
+                return carry
+
+            lax.fori_loop(0, loops, closed, 0)
         else:
             for h in range(loops):
                 body(h, 0)
@@ -203,11 +228,12 @@
         size = GROUP
         for following in sizes:
             before(row0 + size, following, slots[1 - turn])
-            after(row0, size, slots[turn])
+            run(after, row0, size, slots[turn])
             row0, size, turn = row0 + size, following, 1 - turn
-        waiting = functools.partial(after, row0, size, slots[turn])
+        waiting = functools.partial(run, after, row0, size, slots[turn])
         turn = 1 - turn
     waiting()
+    flush()
     for start in range(0, rows_tile, GROUP):
         sent(start).wait()
 

time: 28 us -> 27.4 us (0.979)
  Pallas kernels: 12.2 us -> 11.6 us
    pallas_call x1, Pallas kernels: 10.3 us -> 9.75 us  [call_trunk(): pl.pallas_call(functools.partial(trunk, rows_tile, cols_tile, bins, chann...]
where the time goes in v5:
time: 27.4 us; the launch traced here: 27.2 us
  Pallas kernels  11.6 us (42%)
  starting transfers between devices  7.3 us (27%)
  waiting for transfers between devices  4.98 us (18%)
  local copies, waits for them, and re-layouts  2.92 us (11%)
    pallas_call x1, Pallas kernels, call_trunk(): pl.pallas_call(functools.partial(trunk, rows_tile, cols_tile, bins, chann...  9.75 us
    all_to_all x1, starting transfers between devices, local(): lax.all_to_all(copies, ('row', 'col'), 0, 0).reshape(bins, 2 * channels)  7.3 us
    all_to_all x1, waiting for transfers between devices, local(): lax.all_to_all(copies, ('row', 'col'), 0, 0).reshape(bins, 2 * channels)  4.98 us
    unnamed x9, local copies, waits for them, and re-layouts  1.94 us
    pallas_call x1, Pallas kernels, local(): pl.pallas_call(functools.partial(project, devices), out_shape=jax.ShapeDt...  1.87 us
  transfers between devices with their start and end apart: 1, of which 1 were waited for; matrix products, arithmetic and copies ran while one was open for 4% of the time, Pallas kernels for 0%

profile of v5, /device:TPU:0, one launch (start us, length us, event | category | flops | bytes accessed | tf_op | source)
XLA Modules:
  0.0 27.2 jit_solution(12332751218419135080)
XLA Ops:
  0.0 1.9 %project.1 = bf16[32,16,96]{2,1,0:T(8,128)(2,1)} custom-call(bf16[16,1536]{1,0:T(8,128)(2,1)} %f_ref.1, bf16[48,1536]{1,0:T(8,128)(2,1)} %bitcast.19, bf16[48,1536]{1,0:T(8,128)(2,1)} %bitcast.20), custom_call_target="tpu_custom_call" | custom-call | tf_op jit(solution)/shard_map/project/pallas_call | solution.py:282
  1.9 7.3 %all-to-all-start = ((bf16[32,16,96]{2,1,0:T(8,128)(2,1)}), bf16[32,16,96]{2,1,0:T(8,128)(2,1)S(1)}, u32[]{:S(2)}, u32[]{:S(2)}) async-start(bf16[32,16,96]{2,1,0:T(8,128)(2,1)} %project.1), calls=%async_computation | async-start | bytes 262144 | tf_op jit(solution)/shard_map/all_to_all | solution.py:290
  9.2 0.0 copy-start.3
  9.2 0.6 %copy-done.3 = f32[48]{0:T(128)S(1)} copy-done((f32[48]{0:T(128)S(1)}, f32[48]{0:T(128)}, u32[]{:S(2)}) %copy-start.3) | copy-done | bytes 216
  9.9 0.1 copy.15.bias_ref
  10.0 0.0 copy-start.1
  10.0 0.1 and_select_fusion
  10.0 0.1 select_n.15.hi_ref
  10.2 0.7 %copy-done.1 = bf16[3,3,48,48]{3,2,1,0:T(8,128)(2,1)S(1)} copy-done((bf16[3,3,48,48]{3,2,1,0:T(8,128)(2,1)S(1)}, bf16[3,3,48,48]{3,2,1,0:T(8,128)(2,1)}, u32[]{:S(2)}) %copy-start.1) | copy-done | bytes 41496
  10.9 0.1 maximum_multiply_fusion
  10.9 0.0 copy-start.2
  10.9 0.2 copy.13
  11.1 0.2 mul.20.w1_ref
  11.3 0.6 %copy-done.2 = bf16[3,3,3,48,48]{4,3,2,1,0:T(8,128)(2,1)S(1)} copy-done((bf16[3,3,3,48,48]{4,3,2,1,0:T(8,128)(2,1)S(1)}, bf16[3,3,3,48,48]{4,3,2,1,0:T(8,128)(2,1)}, u32[]{:S(2)}) %copy-start.2) | copy-done | bytes 124440
  11.9 0.2 copy.14
  12.1 0.0 copy-start
  12.1 0.2 reshape.54.wd_ref
  12.3 0.1 pad_add_fusion.pos_ref
  12.4 5.0 %all-to-all-done = bf16[32,16,96]{2,1,0:T(8,128)(2,1)S(1)} async-done(((bf16[32,16,96]{2,1,0:T(8,128)(2,1)}), bf16[32,16,96]{2,1,0:T(8,128)(2,1)S(1)}, u32[]{:S(2)}, u32[]{:S(2)}) %all-to-all-start) | async-done | bytes 98336 | tf_op jit(solution)/shard_map/all_to_all | solution.py:290
  17.4 0.0 copy-done
  17.4 9.8 %trunk.1 = bf16[48,64,128]{2,1,0:T(8,128)(2,1)} custom-call(s32[2]{0:T(128)S(1)} %pad_add_fusion.pos_ref, bf16[512,96]{1,0:T(8,128)(2,1)S(1)} %bitcast.15, bf16[144,288]{1,0:T(8,128)(2,1)S(1)} %mul.20.w1_ref, bf16[3,144,144]{2,1,0:T(8,128)(2,1)S(1)} %reshape.54.wd_ref, bf16[3,48,48]{2,1,0:T(8,128)(2,1)S(1)} %copy-done, f32[48,1]{1,0:T(8,128)S(1)} %copy.15.bias_ref, ...), custom_call_target="tpu_custom_call" | custom-call | tf_op jit(solution)/shard_map/trunk/pallas_call | solution.py:260
  (3 shorter events, 0.0 us)
Async XLA Ops:
  1.9 15.5 %all-to-all-start = ((bf16[32,16,96]{2,1,0:T(8,128)(2,1)}), bf16[32,16,96]{2,1,0:T(8,128)(2,1)S(1)}, u32[]{:S(2)}, u32[]{:S(2)}) async-start(bf16[32,16,96]{2,1,0:T(8,128)(2,1)} %project.1), calls=%async_computation | async-start | bytes 262144 | tf_op jit(solution)/shard_map/all_to_all | solution.py:290
  9.2 0.7 %copy-start.3 = (f32[48]{0:T(128)S(1)}, f32[48]{0:T(128)}, u32[]{:S(2)}) copy-start(f32[48]{0:T(128)} %param.11) | copy-start | bytes 580
  10.0 0.9 %copy-start.1 = (bf16[3,3,48,48]{3,2,1,0:T(8,128)(2,1)S(1)}, bf16[3,3,48,48]{3,2,1,0:T(8,128)(2,1)}, u32[]{:S(2)}) copy-start(bf16[3,3,48,48]{3,2,1,0:T(8,128)(2,1)} %param.10) | copy-start | bytes 124420
  10.9 1.0 %copy-start.2 = (bf16[3,3,3,48,48]{4,3,2,1,0:T(8,128)(2,1)S(1)}, bf16[3,3,3,48,48]{4,3,2,1,0:T(8,128)(2,1)}, u32[]{:S(2)}) copy-start(bf16[3,3,3,48,48]{4,3,2,1,0:T(8,128)(2,1)} %param.12) | copy-start | bytes 373252
  12.1 5.3 %copy-start = (bf16[3,48,48]{2,1,0:T(8,128)(2,1)S(1)}, bf16[3,48,48]{2,1,0:T(8,128)(2,1)}, u32[]{:S(2)}) copy-start(bf16[3,48,48]{2,1,0:T(8,128)(2,1)} %wm_ref.1) | copy-start | bytes 41476

commit v6 on v5

--- a/solution.py
+++ b/solution.py
@@ -46,8 +46,8 @@
         pltpu.VMEM((channels, lanes), jnp.bfloat16),
         pltpu.VMEM((channels, lanes), jnp.bfloat16),
         pltpu.VMEM((channels, LANES), jnp.bfloat16),
-        pltpu.VMEM((channels * PITCH, LANES), jnp.float32),
-        pltpu.VMEM((channels * PITCH, LANES), jnp.float32),
+        pltpu.VMEM(((channels + 1) * PITCH, LANES), jnp.float32),
+        pltpu.VMEM(((channels + 1) * PITCH, LANES), jnp.float32),
         z_shape,
         z_shape,
     )

time: 27.4 us -> 27.4 us (level)
  no operation moved by 1% of the time
where the time goes in v6:
time: 27.4 us; the launch traced here: 27.2 us
  Pallas kernels  11.6 us (42%)
  starting transfers between devices  7.3 us (27%)
  waiting for transfers between devices  4.98 us (18%)
  local copies, waits for them, and re-layouts  2.92 us (11%)
    pallas_call x1, Pallas kernels, call_trunk(): pl.pallas_call(functools.partial(trunk, rows_tile, cols_tile, bins, chann...  9.77 us
    all_to_all x1, starting transfers between devices, local(): lax.all_to_all(copies, ('row', 'col'), 0, 0).reshape(bins, 2 * channels)  7.3 us
    all_to_all x1, waiting for transfers between devices, local(): lax.all_to_all(copies, ('row', 'col'), 0, 0).reshape(bins, 2 * channels)  4.98 us
    unnamed x9, local copies, waits for them, and re-layouts  1.94 us
    pallas_call x1, Pallas kernels, local(): pl.pallas_call(functools.partial(project, devices), out_shape=jax.ShapeDt...  1.87 us
  transfers between devices with their start and end apart: 1, of which 1 were waited for; matrix products, arithmetic and copies ran while one was open for 4% of the time, Pallas kernels for 0%

profile of v6, /device:TPU:0, one launch (start us, length us, event | category | flops | bytes accessed | tf_op | source)
XLA Modules:
  0.0 27.2 jit_solution(18182538932037446297)
XLA Ops:
  0.0 1.9 %project.1 = bf16[32,16,96]{2,1,0:T(8,128)(2,1)} custom-call(bf16[16,1536]{1,0:T(8,128)(2,1)} %f_ref.1, bf16[48,1536]{1,0:T(8,128)(2,1)} %bitcast.19, bf16[48,1536]{1,0:T(8,128)(2,1)} %bitcast.20), custom_call_target="tpu_custom_call" | custom-call | tf_op jit(solution)/shard_map/project/pallas_call | solution.py:282
  1.9 7.3 %all-to-all-start = ((bf16[32,16,96]{2,1,0:T(8,128)(2,1)}), bf16[32,16,96]{2,1,0:T(8,128)(2,1)S(1)}, u32[]{:S(2)}, u32[]{:S(2)}) async-start(bf16[32,16,96]{2,1,0:T(8,128)(2,1)} %project.1), calls=%async_computation | async-start | bytes 262144 | tf_op jit(solution)/shard_map/all_to_all | solution.py:290
  9.2 0.0 copy-start.3
  9.2 0.6 %copy-done.3 = f32[48]{0:T(128)S(1)} copy-done((f32[48]{0:T(128)S(1)}, f32[48]{0:T(128)}, u32[]{:S(2)}) %copy-start.3) | copy-done | bytes 216
  9.9 0.1 copy.15.bias_ref
  10.0 0.0 copy-start.1
  10.0 0.1 and_select_fusion
  10.0 0.1 select_n.15.hi_ref
  10.2 0.7 %copy-done.1 = bf16[3,3,48,48]{3,2,1,0:T(8,128)(2,1)S(1)} copy-done((bf16[3,3,48,48]{3,2,1,0:T(8,128)(2,1)S(1)}, bf16[3,3,48,48]{3,2,1,0:T(8,128)(2,1)}, u32[]{:S(2)}) %copy-start.1) | copy-done | bytes 41496
  10.9 0.1 maximum_multiply_fusion
  10.9 0.0 copy-start.2
  10.9 0.2 copy.13
  11.1 0.2 mul.20.w1_ref
  11.3 0.6 %copy-done.2 = bf16[3,3,3,48,48]{4,3,2,1,0:T(8,128)(2,1)S(1)} copy-done((bf16[3,3,3,48,48]{4,3,2,1,0:T(8,128)(2,1)S(1)}, bf16[3,3,3,48,48]{4,3,2,1,0:T(8,128)(2,1)}, u32[]{:S(2)}) %copy-start.2) | copy-done | bytes 124440
  11.9 0.2 copy.14
  12.1 0.0 copy-start
  12.1 0.2 reshape.54.wd_ref
  12.3 0.1 pad_add_fusion.pos_ref
  12.4 5.0 %all-to-all-done = bf16[32,16,96]{2,1,0:T(8,128)(2,1)S(1)} async-done(((bf16[32,16,96]{2,1,0:T(8,128)(2,1)}), bf16[32,16,96]{2,1,0:T(8,128)(2,1)S(1)}, u32[]{:S(2)}, u32[]{:S(2)}) %all-to-all-start) | async-done | bytes 98336 | tf_op jit(solution)/shard_map/all_to_all | solution.py:290
  17.4 0.0 copy-done
  17.4 9.8 %trunk.1 = bf16[48,64,128]{2,1,0:T(8,128)(2,1)} custom-call(s32[2]{0:T(128)S(1)} %pad_add_fusion.pos_ref, bf16[512,96]{1,0:T(8,128)(2,1)S(1)} %bitcast.15, bf16[144,288]{1,0:T(8,128)(2,1)S(1)} %mul.20.w1_ref, bf16[3,144,144]{2,1,0:T(8,128)(2,1)S(1)} %reshape.54.wd_ref, bf16[3,48,48]{2,1,0:T(8,128)(2,1)S(1)} %copy-done, f32[48,1]{1,0:T(8,128)S(1)} %copy.15.bias_ref, ...), custom_call_target="tpu_custom_call" | custom-call | tf_op jit(solution)/shard_map/trunk/pallas_call | solution.py:260
  (3 shorter events, 0.0 us)
Async XLA Ops:
  1.9 15.5 %all-to-all-start = ((bf16[32,16,96]{2,1,0:T(8,128)(2,1)}), bf16[32,16,96]{2,1,0:T(8,128)(2,1)S(1)}, u32[]{:S(2)}, u32[]{:S(2)}) async-start(bf16[32,16,96]{2,1,0:T(8,128)(2,1)} %project.1), calls=%async_computation | async-start | bytes 262144 | tf_op jit(solution)/shard_map/all_to_all | solution.py:290
  9.2 0.7 %copy-start.3 = (f32[48]{0:T(128)S(1)}, f32[48]{0:T(128)}, u32[]{:S(2)}) copy-start(f32[48]{0:T(128)} %param.11) | copy-start | bytes 580
  10.0 0.9 %copy-start.1 = (bf16[3,3,48,48]{3,2,1,0:T(8,128)(2,1)S(1)}, bf16[3,3,48,48]{3,2,1,0:T(8,128)(2,1)}, u32[]{:S(2)}) copy-start(bf16[3,3,48,48]{3,2,1,0:T(8,128)(2,1)} %param.10) | copy-start | bytes 124420
  10.9 1.0 %copy-start.2 = (bf16[3,3,3,48,48]{4,3,2,1,0:T(8,128)(2,1)S(1)}, bf16[3,3,3,48,48]{4,3,2,1,0:T(8,128)(2,1)}, u32[]{:S(2)}) copy-start(bf16[3,3,3,48,48]{4,3,2,1,0:T(8,128)(2,1)} %param.12) | copy-start | bytes 373252
  12.1 5.3 %copy-start = (bf16[3,48,48]{2,1,0:T(8,128)(2,1)S(1)}, bf16[3,48,48]{2,1,0:T(8,128)(2,1)}, u32[]{:S(2)}) copy-start(bf16[3,48,48]{2,1,0:T(8,128)(2,1)} %wm_ref.1) | copy-start | bytes 41476
